TPU v7x, 128 devices: a whole 4x4x4 slice. The times are simulated.
128 devices in a mesh: samp: 32 (over y, z, core), layer: 4 (over x).
Axes of the slice: x: 4, y: 4, z: 4, core: 2. Of those that a mesh axis runs over, the one named last changes fastest.
Arguments:
- spins: int32 [256, 256], P('samp'), may hold values 0 or 1
- activations: bfloat16 [256, 8, 256, 256], P('samp', 'layer'), may hold values from -6 to 6
- cotangents: bfloat16 [256, 8, 256, 256], P('samp', 'layer'), may hold values from -0.023925781 to 0.023925781
- offdiag: float32 [256], P('samp'), may hold values from -24 to 24
Outputs:
- weights: float32 [256], P('samp')
- update: float32 [8, 256, 256], P('layer', 'samp')
All inputs are finite; a program needn't handle non-finite values. No bound on the sum of `spins` on one device may be relied on, other than what follows from the above.
Results may differ from a plain program's by a relative error of at most 0.0029.
Values may be sent and summed in bfloat16 or wider, within the bound.
A program may use at most 64 MiB of HBM per device.

v0:
```python
import jax
import jax.numpy as jnp
from jax import lax
from jax.sharding import PartitionSpec as P

SIDE = 16


shift_ratio = 0.1
highest = lax.Precision.HIGHEST


def laid_out(parts, dim):
    parts = jnp.moveaxis(parts, 0, dim)
    dims = parts.shape
    return parts.reshape(*dims[:dim], dims[dim] * dims[dim + 1], *dims[dim + 2 :])


def copy_for_each(shard, axis):
    length = lax.axis_size(axis)
    return lax.all_to_all(
        jnp.broadcast_to(shard[None], (length, *shard.shape)), axis, 0, 0, tiled=True
    )


def gather_directly(shard, axis, dim):
    return laid_out(copy_for_each(shard, axis), dim)


def local_energy(spins, offdiag):
    zvals = (2 * spins - 1).astype(jnp.float32).reshape(spins.shape[0], SIDE, SIDE)
    bonds = zvals * jnp.roll(zvals, -1, 2) + zvals * jnp.roll(zvals, -1, 1)
    return offdiag + jnp.sum(bonds, axis=(1, 2))


def small_factor(matrix):
    order = matrix.shape[0]
    positions = lax.iota(jnp.int32, order)

    def one_column(j, carry):
        rest, lower = carry
        column = lax.dynamic_slice_in_dim(rest, j, 1, 1)[:, 0]
        pivot = jnp.sqrt(lax.dynamic_slice_in_dim(column, j, 1)[0])
        scaled = jnp.where(positions >= j, column / pivot, jnp.float32(0.0))
        lower = lax.dynamic_update_slice_in_dim(lower, scaled[:, None], j, 1)
        rest = rest - scaled[:, None] * scaled[None, :]
        return (rest, lower)

    start = (matrix, jnp.zeros_like(matrix))
    return lax.fori_loop(0, order, one_column, start)[1]


def lower_inverse(lower):
    order = lower.shape[0]
    ident = jnp.eye(order, dtype=jnp.float32)

    def one_row(i, inverse):
        lower_row = lax.dynamic_slice_in_dim(lower, i, 1, 0)
        unit_row = lax.dynamic_slice_in_dim(ident, i, 1, 0)
        diag_entry = lax.dynamic_slice_in_dim(lower_row[0], i, 1)[0]
        known = jnp.dot(lower_row, inverse, precision=highest)
        fresh = (unit_row - known) / diag_entry
        return lax.dynamic_update_slice_in_dim(inverse, fresh, i, 0)

    return lax.fori_loop(0, order, one_row, jnp.zeros_like(lower))


def blocked_solve(matrix, rhs):
    block = matrix.shape[0] // 8
    lower_tiles = {}
    inverses = []
    for k in range(8):
        diag_tile = matrix[k * block : (k + 1) * block, k * block : (k + 1) * block]
        for c in range(k):
            diag_tile = diag_tile - jnp.dot(
                lower_tiles[k, c], lower_tiles[k, c].T, precision=highest
            )
        factor = small_factor(diag_tile)
        inverse = lower_inverse(factor)
        inverses.append(inverse)
        for r in range(k + 1, 8):
            tile = matrix[r * block : (r + 1) * block, k * block : (k + 1) * block]
            for c in range(k):
                tile = tile - jnp.dot(lower_tiles[r, c], lower_tiles[k, c].T, precision=highest)
            lower_tiles[r, k] = jnp.dot(tile, inverse.T, precision=highest)
    forward = []
    for k in range(8):
        piece = rhs[k * block : (k + 1) * block]
        for c in range(k):
            piece = piece - jnp.dot(lower_tiles[k, c], forward[c], precision=highest)
        forward.append(jnp.dot(inverses[k], piece, precision=highest))
    backward = [None] * 8
    for k in range(7, -1, -1):
        piece = forward[k]
        for r in range(k + 1, 8):
            piece = piece - jnp.dot(lower_tiles[r, k].T, backward[r], precision=highest)
        backward[k] = jnp.dot(inverses[k].T, piece, precision=highest)
    return jnp.concatenate(backward)


def body(spins, activations, cotangents, offdiag):
    s_local = spins.shape[0]
    energy_local = local_energy(spins, offdiag)
    energy = gather_directly(energy_local, "samp", 0)
    total = energy.shape[0]
    eps = (energy - jnp.mean(energy)) / jnp.sqrt(jnp.float32(total))
    jac = jnp.einsum(
        "ksad,ksae->ksde", activations, cotangents, preferred_element_type=jnp.float32
    ).astype(jnp.bfloat16)
    regrouped = lax.all_to_all(jac, "samp", split_axis=2, concat_axis=0, tiled=True)
    flat = regrouped.reshape(total, -1)
    col_mean = jnp.mean(flat, axis=0, dtype=jnp.float32)
    raw_gram = jnp.dot(flat, flat.T, preferred_element_type=jnp.float32)
    row_dots = jnp.dot(flat.astype(jnp.float32), col_mean, precision=highest)
    mean_square = jnp.sum(col_mean * col_mean)
    partial_value = (raw_gram - row_dots[:, None] - row_dots[None, :] + mean_square) / total
    gram = lax.psum(partial_value, ("samp", "layer"))
    shift = shift_ratio * jnp.trace(gram) / total
    weights = blocked_solve(gram + shift * jnp.eye(total, dtype=jnp.float32), eps)
    start = lax.axis_index("samp") * s_local
    own_weights = lax.dynamic_slice_in_dim(weights, start, s_local)
    coeffs_all = weights - jnp.mean(weights)
    update = jnp.dot(coeffs_all, flat.astype(jnp.float32), precision=highest).reshape(
        regrouped.shape[1:]
    )
    return (own_weights, update)


def solution(mesh):
    placed = (
        P("samp", None),
        P("samp", "layer", None, None),
        P("samp", "layer", None, None),
        P("samp"),
    )
    return jax.shard_map(
        body,
        mesh=mesh,
        in_specs=placed,
        out_specs=(P("samp"), P("layer", "samp", None)),
        check_vma=False,
    )
```

profile of v0, /device:TPU:1, one launch (start us, length us, event | category | flops | bytes accessed | tf_op | source)
XLA Modules:
  0.0 995.8 jit_solution(18253489442866644126)
XLA Ops:
  10.5 9.6 all-to-all-start.1
  20.1 2.4 convolution_convert_fusion
  22.5 3.5 copy.85
  25.9 1.0 all-to-all-done.1
  27.0 6.4 all-to-all-start
  34.7 27.0 %all-to-all-done = bf16[8,2,256,256]{3,1,0,2:T(2,128)(2,1)} async-done(((bf16[8,2,256,256]{3,1,0,2:T(2,128)(2,1)}), bf16[8,2,256,256]{3,1,0,2:T(2,128)(2,1)}, u32[]{:S(2)}, u32[]{:S(2)}) %all-to-all-start) | async-done | bytes 2097184 | tf_op jit(solution)/shard_map/all_to_all | solution.py:110
  61.7 2.8 convert_reduce_fusion
  64.5 4.2 copy.135
  68.8 4.2 reshape.493
  73.6 3.5 fusion.238
  77.1 2.1 fusion.52
  79.9 3.6 copy.128
  83.5 134.9 %all-reduce.2.cloned.1.call-done = f32[256,256]{1,0:T(8,128)} async-done(((f32[256,256]{1,0:T(8,128)}), f32[256,256]{1,0:T(8,128)}) %all-reduce.2.cloned.1.call-update) | async-done | bytes 262160 | tf_op jit(solution)/shard_map/psum | solution.py:117
  218.4 1.6 select_reduce_fusion
  220.6 1.0 select_add_fusion
  221.7 44.8 %while.288 = (s32[]{:T(128)}, f32[32,32]{0,1:T(8,128)S(1)}, f32[32,32]{0,1:T(8,128)S(1)}, s32[]{:T(128)}, s32[]{:T(128)}, /*index=5*/s32[]{:T(128)}) while((s32[]{:T(128)}, f32[32,32]{0,1:T(8,128)S(1)}, f32[32,32]{0,1:T(8,128)S(1)}, s32[]{:T(128)}, s32[]{:T(128)}, /*index=5*/s32[]{:T(128)}) %tuple.681), condition=%wide.region_5.6_spmd.clone, body=%wide.region_4.5_spmd.clone.sunk | while | flops 2211 | bytes 10493 | solution.py:50
  266.6 45.1 %while.280 = (s32[]{:T(128)}, f32[32,32]{1,0:T(8,128)S(1)}, f32[32,32]{1,0:T(8,128)S(1)}, f32[32,32]{1,0:T(8,128)S(1)}, s32[]{:T(128)}, /*index=5*/s32[]{:T(128)}, s32[]{:T(128)}) while((s32[]{:T(128)}, f32[32,32]{1,0:T(8,128)S(1)}, f32[32,32]{1,0:T(8,128)S(1)}, f32[32,32]{1,0:T(8,128)S(1)}, s32[]{:T(128)}, /*index=5*/s32[]{:T(128)}, ...), condition=%wide.region_7.8_spmd, body=%wide.region_6.7_spmd.sunk | while | flops 12355 | bytes 18937 | solution.py:65
  318.4 45.6 %while.289 = (s32[]{:T(128)}, f32[32,32]{0,1:T(8,128)S(1)}, f32[32,32]{0,1:T(8,128)S(1)}, s32[]{:T(128)}, s32[]{:T(128)}, /*index=5*/s32[]{:T(128)}) while((s32[]{:T(128)}, f32[32,32]{0,1:T(8,128)S(1)}, f32[32,32]{0,1:T(8,128)S(1)}, s32[]{:T(128)}, s32[]{:T(128)}, /*index=5*/s32[]{:T(128)}) %tuple.687), condition=%wide.region_11.12_spmd.clone, body=%wide.region_10.11_spmd.clone.sunk | while | flops 2211 | bytes 10493 | solution.py:50
  364.0 45.1 %while.281 = (s32[]{:T(128)}, f32[32,32]{1,0:T(8,128)S(1)}, f32[32,32]{1,0:T(8,128)S(1)}, f32[32,32]{1,0:T(8,128)S(1)}, s32[]{:T(128)}, /*index=5*/s32[]{:T(128)}, s32[]{:T(128)}) while((s32[]{:T(128)}, f32[32,32]{1,0:T(8,128)S(1)}, f32[32,32]{1,0:T(8,128)S(1)}, f32[32,32]{1,0:T(8,128)S(1)}, s32[]{:T(128)}, /*index=5*/s32[]{:T(128)}, ...), condition=%wide.region_13.14_spmd, body=%wide.region_12.13_spmd.sunk | while | flops 12355 | bytes 18937 | solution.py:65
  412.9 45.5 %while.290 = (s32[]{:T(128)}, f32[32,32]{0,1:T(8,128)S(1)}, f32[32,32]{0,1:T(8,128)S(1)}, s32[]{:T(128)}, s32[]{:T(128)}, /*index=5*/s32[]{:T(128)}) while((s32[]{:T(128)}, f32[32,32]{0,1:T(8,128)S(1)}, f32[32,32]{0,1:T(8,128)S(1)}, s32[]{:T(128)}, s32[]{:T(128)}, /*index=5*/s32[]{:T(128)}) %tuple.693), condition=%wide.region_15.16_spmd.clone, body=%wide.region_14.15_spmd.clone.sunk | while | flops 2211 | bytes 10493 | solution.py:50
  458.5 45.1 %while.282 = (s32[]{:T(128)}, f32[32,32]{1,0:T(8,128)S(1)}, f32[32,32]{1,0:T(8,128)S(1)}, f32[32,32]{1,0:T(8,128)S(1)}, s32[]{:T(128)}, /*index=5*/s32[]{:T(128)}, s32[]{:T(128)}) while((s32[]{:T(128)}, f32[32,32]{1,0:T(8,128)S(1)}, f32[32,32]{1,0:T(8,128)S(1)}, f32[32,32]{1,0:T(8,128)S(1)}, s32[]{:T(128)}, /*index=5*/s32[]{:T(128)}, ...), condition=%wide.region_17.18_spmd, body=%wide.region_16.17_spmd.sunk | while | flops 12355 | bytes 18937 | solution.py:65
  507.4 45.5 %while.291 = (s32[]{:T(128)}, f32[32,32]{0,1:T(8,128)S(1)}, f32[32,32]{0,1:T(8,128)S(1)}, s32[]{:T(128)}, s32[]{:T(128)}, /*index=5*/s32[]{:T(128)}) while((s32[]{:T(128)}, f32[32,32]{0,1:T(8,128)S(1)}, f32[32,32]{0,1:T(8,128)S(1)}, s32[]{:T(128)}, s32[]{:T(128)}, /*index=5*/s32[]{:T(128)}) %tuple.699), condition=%wide.region_19.20_spmd.clone, body=%wide.region_18.19_spmd.clone.sunk | while | flops 2211 | bytes 10493 | solution.py:50
  553.0 45.1 %while.283 = (s32[]{:T(128)}, f32[32,32]{1,0:T(8,128)S(1)}, f32[32,32]{1,0:T(8,128)S(1)}, f32[32,32]{1,0:T(8,128)S(1)}, s32[]{:T(128)}, /*index=5*/s32[]{:T(128)}, s32[]{:T(128)}) while((s32[]{:T(128)}, f32[32,32]{1,0:T(8,128)S(1)}, f32[32,32]{1,0:T(8,128)S(1)}, f32[32,32]{1,0:T(8,128)S(1)}, s32[]{:T(128)}, /*index=5*/s32[]{:T(128)}, ...), condition=%wide.region_21.22_spmd, body=%wide.region_20.21_spmd.sunk | while | flops 12355 | bytes 18937 | solution.py:65
  601.6 45.5 %while.292 = (s32[]{:T(128)}, f32[32,32]{0,1:T(8,128)S(1)}, f32[32,32]{0,1:T(8,128)S(1)}, s32[]{:T(128)}, s32[]{:T(128)}, /*index=5*/s32[]{:T(128)}) while((s32[]{:T(128)}, f32[32,32]{0,1:T(8,128)S(1)}, f32[32,32]{0,1:T(8,128)S(1)}, s32[]{:T(128)}, s32[]{:T(128)}, /*index=5*/s32[]{:T(128)}) %tuple.705), condition=%wide.region_23.24_spmd.clone, body=%wide.region_22.23_spmd.clone.sunk | while | flops 2211 | bytes 10493 | solution.py:50
  647.2 45.1 %while.284 = (s32[]{:T(128)}, f32[32,32]{1,0:T(8,128)S(1)}, f32[32,32]{1,0:T(8,128)S(1)}, f32[32,32]{1,0:T(8,128)S(1)}, s32[]{:T(128)}, /*index=5*/s32[]{:T(128)}, s32[]{:T(128)}) while((s32[]{:T(128)}, f32[32,32]{1,0:T(8,128)S(1)}, f32[32,32]{1,0:T(8,128)S(1)}, f32[32,32]{1,0:T(8,128)S(1)}, s32[]{:T(128)}, /*index=5*/s32[]{:T(128)}, ...), condition=%wide.region_25.26_spmd, body=%wide.region_24.25_spmd.sunk | while | flops 12355 | bytes 18937 | solution.py:65
  695.8 45.5 %while.293 = (s32[]{:T(128)}, f32[32,32]{0,1:T(8,128)S(1)}, f32[32,32]{0,1:T(8,128)S(1)}, s32[]{:T(128)}, s32[]{:T(128)}, /*index=5*/s32[]{:T(128)}) while((s32[]{:T(128)}, f32[32,32]{0,1:T(8,128)S(1)}, f32[32,32]{0,1:T(8,128)S(1)}, s32[]{:T(128)}, s32[]{:T(128)}, /*index=5*/s32[]{:T(128)}) %tuple.711), condition=%wide.region_27.28_spmd.clone, body=%wide.region_26.27_spmd.clone.sunk | while | flops 2211 | bytes 10493 | solution.py:50
  741.4 45.1 %while.285 = (s32[]{:T(128)}, f32[32,32]{1,0:T(8,128)S(1)}, f32[32,32]{1,0:T(8,128)S(1)}, f32[32,32]{1,0:T(8,128)S(1)}, s32[]{:T(128)}, /*index=5*/s32[]{:T(128)}, s32[]{:T(128)}) while((s32[]{:T(128)}, f32[32,32]{1,0:T(8,128)S(1)}, f32[32,32]{1,0:T(8,128)S(1)}, f32[32,32]{1,0:T(8,128)S(1)}, s32[]{:T(128)}, /*index=5*/s32[]{:T(128)}, ...), condition=%wide.region_29.30_spmd, body=%wide.region_28.29_spmd.sunk | while | flops 12355 | bytes 18937 | solution.py:65
  787.8 45.5 %while.294 = (s32[]{:T(128)}, f32[32,32]{0,1:T(8,128)S(1)}, f32[32,32]{0,1:T(8,128)S(1)}, s32[]{:T(128)}, s32[]{:T(128)}, /*index=5*/s32[]{:T(128)}) while((s32[]{:T(128)}, f32[32,32]{0,1:T(8,128)S(1)}, f32[32,32]{0,1:T(8,128)S(1)}, s32[]{:T(128)}, s32[]{:T(128)}, /*index=5*/s32[]{:T(128)}) %tuple.717), condition=%wide.region_31.32_spmd.clone, body=%wide.region_30.31_spmd.clone.sunk | while | flops 2211 | bytes 10493 | solution.py:50
  833.4 45.1 %while.286 = (s32[]{:T(128)}, f32[32,32]{1,0:T(8,128)S(1)}, f32[32,32]{1,0:T(8,128)S(1)}, f32[32,32]{1,0:T(8,128)S(1)}, s32[]{:T(128)}, /*index=5*/s32[]{:T(128)}, s32[]{:T(128)}) while((s32[]{:T(128)}, f32[32,32]{1,0:T(8,128)S(1)}, f32[32,32]{1,0:T(8,128)S(1)}, f32[32,32]{1,0:T(8,128)S(1)}, s32[]{:T(128)}, /*index=5*/s32[]{:T(128)}, ...), condition=%wide.region_33.34_spmd, body=%wide.region_32.33_spmd.sunk | while | flops 12355 | bytes 18937 | solution.py:65
  879.0 45.5 %while.295 = (s32[]{:T(128)}, f32[32,32]{0,1:T(8,128)S(1)}, f32[32,32]{0,1:T(8,128)S(1)}, s32[]{:T(128)}, s32[]{:T(128)}, /*index=5*/s32[]{:T(128)}) while((s32[]{:T(128)}, f32[32,32]{0,1:T(8,128)S(1)}, f32[32,32]{0,1:T(8,128)S(1)}, s32[]{:T(128)}, s32[]{:T(128)}, /*index=5*/s32[]{:T(128)}) %tuple.723), condition=%wide.region_35.36_spmd.clone, body=%wide.region_34.35_spmd.clone.sunk | while | flops 2211 | bytes 10493 | solution.py:50
  924.6 45.1 %while.287 = (s32[]{:T(128)}, f32[32,32]{1,0:T(8,128)S(1)}, f32[32,32]{1,0:T(8,128)S(1)}, f32[32,32]{1,0:T(8,128)S(1)}, s32[]{:T(128)}, /*index=5*/s32[]{:T(128)}, s32[]{:T(128)}) while((s32[]{:T(128)}, f32[32,32]{1,0:T(8,128)S(1)}, f32[32,32]{1,0:T(8,128)S(1)}, f32[32,32]{1,0:T(8,128)S(1)}, s32[]{:T(128)}, /*index=5*/s32[]{:T(128)}, ...), condition=%wide.region_37.38_spmd, body=%wide.region_36.37_spmd.sunk | while | flops 12355 | bytes 18937 | solution.py:65
  985.5 2.8 fusion.48
  (2299 shorter events, 577.6 us)
Async XLA Ops:
  7.2 13.0 %copy-start = (bf16[8,2,256,256]{3,2,1,0:T(8,128)(2,1)S(1)}, bf16[8,2,256,256]{3,2,1,0:T(8,128)(2,1)}, u32[]{:S(2)}) copy-start(bf16[8,2,256,256]{3,2,1,0:T(8,128)(2,1)} %param.37) | copy-start | bytes 6291460
  10.5 16.5 %all-to-all-start.1 = ((f32[32,1,8]{2,1,0:T(1,128)}), f32[32,1,8]{2,1,0:T(1,128)S(1)}, u32[]{:S(2)}, u32[]{:S(2)}) async-start(f32[32,1,8]{2,1,0:T(1,128)} %broadcast_in_dim.126), calls=%async_computation.1 | async-start | bytes 32768 | tf_op jit(solution)/shard_map/all_to_all | solution.py:21
  27.0 34.8 %all-to-all-start = ((bf16[8,2,256,256]{3,1,0,2:T(2,128)(2,1)}), bf16[8,2,256,256]{3,1,0,2:T(2,128)(2,1)}, u32[]{:S(2)}, u32[]{:S(2)}) async-start(bf16[8,2,256,256]{3,1,0,2:T(2,128)(2,1)} %copy.85), calls=%async_computation | async-start | bytes 4194304 | tf_op jit(solution)/shard_map/all_to_all | solution.py:110
  33.4 185.0 %all-reduce.2.cloned.1.call-start = ((), (), s32[]{:S(2)}) async-start(), calls=%async_computation.2 | async-start | bytes 524288 | tf_op jit(solution)/shard_map/psum | solution.py:117
  73.6 3.5 copy-start.1
Sparse Core Ops, SparseCore 0:
  79.3 139.0 all-reduce.1
where the time goes:
time: 1000 us; the launch traced here: 996 us
  local copies, waits for them, and re-layouts  334 us (33%)
  matrix products  242 us (24%)
  loops' own time  186 us (19%)
  waiting for transfers between devices  163 us (16%)
  other arithmetic  32.5 us (3%)
  between operations  21.3 us (2%)
  starting transfers between devices  16 us (2%)
    dot_general x256, matrix products, one_row(): known = jnp.dot(lower_row, inverse, precision=highest)  200 us
    another operation x8, loops' own time, small_factor(): return lax.fori_loop(0, order, one_column, start)[1]  183 us
    dynamic_slice x256, local copies, waits for them, and re-layouts, one_column(): pivot = jnp.sqrt(lax.dynamic_slice_in_dim(column, j, 1)[0])  151 us
    dynamic_slice x256, local copies, waits for them, and re-layouts, one_row(): diag_entry = lax.dynamic_slice_in_dim(lower_row[0], i, 1)[0]  151 us
    psum x1, waiting for transfers between devices, body(): gram = lax.psum(partial_value, ('samp', 'layer'))  135 us
    all_to_all x1, waiting for transfers between devices, body(): lax.all_to_all(jac, 'samp', split_axis=2, concat_axis=0, tiled=True)  27 us
  transfers between devices with their start and end apart: 3, of which 3 were waited for; matrix products, arithmetic and copies ran while one was open for 1% of the time, Pallas kernels for 0%

commit v1 on v0

v1 whole, which is shorter than its diff:
```python
import functools

import jax
import jax.numpy as jnp
from jax import lax
from jax.experimental import pallas as pl
from jax.experimental.pallas import tpu as pltpu
from jax.sharding import PartitionSpec as P

SIDE = 16


shift_ratio = 0.1
highest = lax.Precision.HIGHEST


def laid_out(parts, dim):
    parts = jnp.moveaxis(parts, 0, dim)
    dims = parts.shape
    return parts.reshape(*dims[:dim], dims[dim] * dims[dim + 1], *dims[dim + 2 :])


def copy_for_each(shard, axis):
    length = lax.axis_size(axis)
    return lax.all_to_all(
        jnp.broadcast_to(shard[None], (length, *shard.shape)), axis, 0, 0, tiled=True
    )


def gather_directly(shard, axis, dim):
    return laid_out(copy_for_each(shard, axis), dim)


def local_energy(spins, offdiag):
    zvals = (2 * spins - 1).astype(jnp.float32).reshape(spins.shape[0], SIDE, SIDE)
    bonds = zvals * jnp.roll(zvals, -1, 2) + zvals * jnp.roll(zvals, -1, 1)
    return offdiag + jnp.sum(bonds, axis=(1, 2))


def tile_inverse(tile):
    order = tile.shape[0]
    sub = lax.broadcasted_iota(jnp.int32, (order, order), 0)
    lane = lax.broadcasted_iota(jnp.int32, (order, order), 1)
    sub_col = lax.broadcasted_iota(jnp.int32, (order, 1), 0)
    lane_row = lax.broadcasted_iota(jnp.int32, (1, order), 1)
    for k in range(order):
        row = tile[k : k + 1, :]
        col = tile[:, k : k + 1]
        inv_pivot = 1.0 / tile[k : k + 1, k : k + 1]
        scaled = jnp.where(lane_row == k, 1.0, row) * inv_pivot
        kept = jnp.where((lane == k) | (sub == k), 0.0, tile)
        tile = kept - jnp.where(sub_col == k, -1.0, col) * scaled
    return tile


def solve_kernel(block, gram_ref, rhs_ref, out_ref, work):
    order = gram_ref.shape[0]
    work[0:order, :] = gram_ref[...]
    work[order : order + 8, :] = jnp.broadcast_to(rhs_ref[...], (8, order))
    lane = lax.broadcasted_iota(jnp.int32, (1, order), 1)
    for k in range(order // block):
        own = slice(k * block, (k + 1) * block)
        below = slice((k + 1) * block, order + 8)
        inverse = tile_inverse(work[own, own])
        scaled = jnp.dot(work[below, own], inverse, precision=highest, preferred_element_type=jnp.float32)
        inside = (lane >= k * block) & (lane < (k + 1) * block)
        pivot_rows = jnp.where(inside, 0.0, work[own, :])
        work[below, :] = work[below, :] - jnp.dot(
            scaled, pivot_rows, precision=highest, preferred_element_type=jnp.float32
        )
        work[below, own] = scaled
    out_ref[...] = work[order : order + 1, :]


def solve(matrix, rhs):
    order = matrix.shape[0]
    return pl.pallas_call(
        functools.partial(solve_kernel, 64),
        out_shape=jax.ShapeDtypeStruct((1, order), jnp.float32),
        in_specs=[pl.BlockSpec(memory_space=pltpu.VMEM)] * 2,
        out_specs=pl.BlockSpec(memory_space=pltpu.VMEM),
        scratch_shapes=[pltpu.VMEM((order + 8, order), jnp.float32)],
    )(matrix, rhs[None, :])[0]


def sum_directly(partial_sum, axes):
    devices = 1
    for axis in axes:
        devices = devices * lax.axis_size(axis)
    rows = partial_sum.shape[0] // devices
    pieces = lax.all_to_all(
        partial_sum.reshape(devices, rows, -1), axes, 0, 0, tiled=True
    )
    own = jnp.sum(pieces, axis=0)
    spread = lax.all_to_all(
        jnp.broadcast_to(own[None], pieces.shape), axes, 0, 0, tiled=True
    )
    return spread.reshape(partial_sum.shape)


def body(spins, activations, cotangents, offdiag):
    s_local = spins.shape[0]
    energy_local = local_energy(spins, offdiag)
    energy = gather_directly(energy_local, "samp", 0)
    total = energy.shape[0]
    eps = (energy - jnp.mean(energy)) / jnp.sqrt(jnp.float32(total))
    jac = jnp.einsum(
        "ksad,ksae->ksde", activations, cotangents, preferred_element_type=jnp.float32
    ).astype(jnp.bfloat16)
    regrouped = lax.all_to_all(jac, "samp", split_axis=2, concat_axis=0, tiled=True)
    flat = regrouped.reshape(total, -1)
    col_mean = jnp.mean(flat, axis=0, dtype=jnp.float32)
    raw_gram = jnp.dot(flat, flat.T, preferred_element_type=jnp.float32)
    row_dots = jnp.dot(flat.astype(jnp.float32), col_mean, precision=highest)
    mean_square = jnp.sum(col_mean * col_mean)
    partial_value = (raw_gram - row_dots[:, None] - row_dots[None, :] + mean_square) / total
    gram = sum_directly(partial_value, ("samp", "layer"))
    shift = shift_ratio * jnp.trace(gram) / total
    weights = solve(gram + shift * jnp.eye(total, dtype=jnp.float32), eps)
    start = lax.axis_index("samp") * s_local
    own_weights = lax.dynamic_slice_in_dim(weights, start, s_local)
    coeffs_all = weights - jnp.mean(weights)
    update = jnp.dot(coeffs_all, flat.astype(jnp.float32), precision=highest).reshape(
        regrouped.shape[1:]
    )
    return (own_weights, update)


def solution(mesh):
    placed = (
        P("samp", None),
        P("samp", "layer", None, None),
        P("samp", "layer", None, None),
        P("samp"),
    )
    return jax.shard_map(
        body,
        mesh=mesh,
        in_specs=placed,
        out_specs=(P("samp"), P("layer", "samp", None)),
        check_vma=False,
    )
```

time: 1000 us -> 139 us (0.14)
  local copies, waits for them, and re-layouts: 334 us -> 19.4 us
  matrix products: 242 us -> 10.1 us
  loops' own time: 186 us -> 0 us
  waiting for transfers between devices: 163 us -> 23.3 us
  blocking collectives: 0 us -> 37.6 us
  other arithmetic: 32.5 us -> 5.83 us
  Pallas kernels: 0 us -> 25.2 us
  between operations: 21.3 us -> 2.76 us
    dynamic_slice x512 -> x0, local copies, waits for them, and re-layouts: 302 us -> none  [the longest x256 151 us: one_column(): pivot = jnp.sqrt(lax.dynamic_slice_in_dim(column, j, 1)[0])]
    dot_general x440 -> x0, matrix products: 231 us -> none  [the longest x256 200 us: one_row(): known = jnp.dot(lower_row, inverse, precision=highest)]
    another operation x16 -> x0, loops' own time: 186 us -> none  [the longest x8 183 us: small_factor(): return lax.fori_loop(0, order, one_column, start)[1]]
    psum x1 -> x0, waiting for transfers between devices: 135 us -> none  [body(): gram = lax.psum(partial_value, ('samp', 'layer'))]
    all_to_all x0 -> x1, blocking collectives: none -> 37.6 us  [body(): lax.all_to_all(jac, 'samp', split_axis=2, concat_axis=0, tiled=True)]
    pallas_call x0 -> x1, Pallas kernels: none -> 25.2 us  [solve(): pl.pallas_call(functools.partial(solve_kernel, 64), out_shape=jax.ShapeDt...]
    sub x257 -> x0, other arithmetic: 18.9 us -> none  [the longest x256 18.9 us: one_column(): rest = rest - scaled[:, None] * scaled[None, :]]
    dynamic_update_slice x512 -> x0, local copies, waits for them, and re-layouts: 13.2 us -> none  [the longest x256 6.6 us: one_column(): lower = lax.dynamic_update_slice_in_dim(lower, scaled[:, None], j, 1)]
  transfers between devices with their start and end apart: 3 -> 3, of which waited for: 3 -> 3; matrix products, arithmetic and copies ran while one was open for 1% -> 4% of each run, Pallas kernels for 0% -> 0%
where the time goes in v1:
time: 139 us; the launch traced here: 138 us
  blocking collectives  37.6 us (27%)
  Pallas kernels  25.2 us (18%)
  waiting for transfers between devices  23.3 us (17%)
  local copies, waits for them, and re-layouts  19.4 us (14%)
  starting transfers between devices  14.1 us (10%)
  matrix products  10.1 us (7%)
  other arithmetic  5.83 us (4%)
  between operations  2.76 us (2%)
    all_to_all x1, blocking collectives, body(): lax.all_to_all(jac, 'samp', split_axis=2, concat_axis=0, tiled=True)  37.6 us
    pallas_call x1, Pallas kernels, solve(): pl.pallas_call(functools.partial(solve_kernel, 64), out_shape=jax.ShapeDt...  25.2 us
    all_to_all x1, waiting for transfers between devices, sum_directly(): lax.all_to_all(partial_sum.reshape(devices, rows, -1), axes, 0, 0, tiled=...  10.8 us
    all_to_all x1, waiting for transfers between devices, copy_for_each(): lax.all_to_all(jnp.broadcast_to(shard[None], (length, *shard.shape)), axi...  6.72 us
    all_to_all x1, starting transfers between devices, sum_directly(): lax.all_to_all(partial_sum.reshape(devices, rows, -1), axes, 0, 0, tiled=...  5.85 us
    all_to_all x1, waiting for transfers between devices, sum_directly(): lax.all_to_all(jnp.broadcast_to(own[None], pieces.shape), axes, 0, 0, til...  5.77 us
    unnamed x9, local copies, waits for them, and re-layouts  5.16 us
    reshape x1, local copies, waits for them, and re-layouts, body(): flat = regrouped.reshape(total, -1)  4.2 us
  transfers between devices with their start and end apart: 3, of which 3 were waited for; matrix products, arithmetic and copies ran while one was open for 4% of the time, Pallas kernels for 0%

profile of v1, /device:TPU:1, one launch (start us, length us, event | category | flops | bytes accessed | tf_op | source)
XLA Modules:
  0.0 138.1 jit_solution(7330970454194098756)
XLA Ops:
  0.6 1.6 %copy-done = bf16[8,2,256,256]{3,2,1,0:T(8,128)(2,1)S(1)} copy-done((bf16[8,2,256,256]{3,2,1,0:T(8,128)(2,1)S(1)}, bf16[8,2,256,256]{3,2,1,0:T(8,128)(2,1)}, u32[]{:S(2)}) %copy-start) | copy-done | bytes 2097176
  2.2 2.4 %convolution_convert_fusion = bf16[8,2,256,256]{3,2,1,0:T(8,128)(2,1)S(1)} fusion(bf16[8,2,256,256]{3,2,1,0:T(8,128)(2,1)S(1)} %copy-done, bf16[8,2,256,256]{3,2,1,0:T(8,128)(2,1)} %param.6), kind=kOutput, calls=%fused_computation.4 | convolution fusion | flops 537919488 | bytes 6291456 | tf_op jit(solution)/shard_map/ksad,ksae->ksde/dot_general | solution.py:107
  4.6 2.2 %copy.13 = bf16[8,2,256,256]{3,1,0,2:T(2,128)(2,1)S(1)} copy(bf16[8,2,256,256]{3,2,1,0:T(8,128)(2,1)S(1)} %convolution_convert_fusion) | data formatting | bytes 4194304 | tf_op jit(solution)/shard_map/convert_element_type | solution.py:109
  6.8 37.6 %all_to_all.31 = bf16[8,2,256,256]{3,1,0,2:T(2,128)(2,1)S(1)} all-to-all(bf16[8,2,256,256]{3,1,0,2:T(2,128)(2,1)S(1)} %copy.13), channel_id=1, replica_groups=mesh['samp'=32,'layer'=4] {'samp'}, dimensions={2} | all-to-all | bytes 4194304 | tf_op jit(solution)/shard_map/all_to_all | solution.py:110
  44.3 1.2 convert_reduce_fusion
  45.5 2.6 %copy.26 = bf16[8,2,32,8,256]{4,3,1,0,2:T(8,128)(2,1)} copy(bf16[8,2,32,8,256]{4,1,0,3,2:T(2,128)(2,1)S(1)} %bitcast.36) | data formatting | bytes 4194304 | tf_op jit(solution)/shard_map/all_to_all | solution.py:110
  48.1 4.2 %reshape.69 = bf16[256,4096]{1,0:T(8,128)(2,1)} reshape(bf16[32,8,2,8,256]{4,3,2,1,0:T(8,128)(2,1)} %bitcast.38) | data formatting | bytes 4194304 | tf_op jit(solution)/shard_map/reshape | solution.py:111
  52.3 0.6 broadcast_multiply_fusion
  53.0 3.5 %fusion.9 = f32[1,256]{1,0:T(1,128)S(1)} fusion(bf16[256,4096]{1,0:T(8,128)(2,1)} %reshape.69, f32[4096,1]{0,1:T(1,128)S(1)} %reshape.74), kind=kOutput, calls=%fused_computation.25 | convolution fusion | flops 12582912 | bytes 2114560 | tf_op jit(solution)/shard_map/dot_general | solution.py:114
  56.5 1.4 %fusion.4 = f32[256,256]{1,0:T(8,128)S(1)} fusion(bf16[256,4096]{1,0:T(8,128)(2,1)S(1)} %copy-done.1, f32[]{:T(128)} %get-tuple-element.3, f32[256]{0:T(256)S(1)} %bitcast.41), kind=kOutput, calls=%fused_computation.8 | convolution fusion | flops 537133056 | bytes 2360324 | tf_op jit(solution)/shard_map/dot_general | solution.py:113
  57.9 0.9 reshape.70
  58.7 5.8 %all-to-all-start.1 = ((f32[128,2,256]{2,1,0:T(2,128)}), f32[128,2,256]{2,1,0:T(2,128)S(1)}, u32[]{:S(2)}, u32[]{:S(2)}) async-start(f32[128,2,256]{2,1,0:T(2,128)} %reshape.70), calls=%async_computation.1 | async-start | bytes 524288 | tf_op jit(solution)/shard_map/all_to_all | solution.py:91
  65.0 0.1 multiply_reduce_fusion.2
  65.1 10.8 %all-to-all-done.1 = f32[128,2,256]{2,1,0:T(2,128)S(1)} async-done(((f32[128,2,256]{2,1,0:T(2,128)}), f32[128,2,256]{2,1,0:T(2,128)S(1)}, u32[]{:S(2)}, u32[]{:S(2)}) %all-to-all-start.1) | async-done | bytes 262176 | tf_op jit(solution)/shard_map/all_to_all | solution.py:91
  75.9 0.6 broadcast_in_dim.9
  76.5 4.0 %all-to-all-start.3 = ((f32[32,1,8]{2,1,0:T(1,128)}), f32[32,1,8]{2,1,0:T(1,128)S(1)}, u32[]{:S(2)}, u32[]{:S(2)}) async-start(f32[32,1,8]{2,1,0:T(1,128)} %broadcast_in_dim.9), calls=%async_computation.3 | async-start | bytes 32768 | tf_op jit(solution)/shard_map/all_to_all | solution.py:25
  80.6 0.1 reduce_sum.66
  80.7 6.7 %all-to-all-done.3 = f32[32,1,8]{2,1,0:T(1,128)S(1)} async-done(((f32[32,1,8]{2,1,0:T(1,128)}), f32[32,1,8]{2,1,0:T(1,128)S(1)}, u32[]{:S(2)}, u32[]{:S(2)}) %all-to-all-start.3) | async-done | bytes 1056 | tf_op jit(solution)/shard_map/all_to_all | solution.py:25
  87.4 0.8 broadcast_in_dim.7
  88.2 4.2 %all-to-all-start.2 = ((f32[128,2,256]{2,1,0:T(2,128)}), f32[128,2,256]{2,1,0:T(2,128)S(1)}, u32[]{:S(2)}, u32[]{:S(2)}) async-start(f32[128,2,256]{2,1,0:T(2,128)} %broadcast_in_dim.7), calls=%async_computation.2 | async-start | bytes 524288 | tf_op jit(solution)/shard_map/all_to_all | solution.py:95
  92.4 0.6 reduce_sum.69
  93.8 0.7 div.40.rhs_ref
  94.4 3.5 %copy.19 = bf16[32,8,16,256]{3,2,1,0:T(8,128)(2,1)} copy(bf16[32,8,16,256]{3,1,2,0:T(8,128)(2,1)} %bitcast.34) | data formatting | bytes 4194304
  98.0 5.8 %all-to-all-done.2 = f32[128,2,256]{2,1,0:T(2,128)S(1)} async-done(((f32[128,2,256]{2,1,0:T(2,128)}), f32[128,2,256]{2,1,0:T(2,128)S(1)}, u32[]{:S(2)}, u32[]{:S(2)}) %all-to-all-start.2) | async-done | bytes 262176 | tf_op jit(solution)/shard_map/all_to_all | solution.py:95
  103.7 1.0 fusion.5
  105.4 0.2 reshape.71
  105.5 0.7 select_add_fusion.gram_ref
  106.3 25.2 %shard_map.59 = f32[1,256]{1,0:T(1,128)} custom-call(f32[256,256]{1,0:T(8,128)} %select_add_fusion.gram_ref, f32[1,256]{1,0:T(1,128)} %div.40.rhs_ref), custom_call_target="tpu_custom_call" | custom-call | tf_op jit(solution)/shard_map/pallas_call | solution.py:77
  131.4 1.3 reduce_sum.70
  133.4 1.3 dynamic-slice_bitcast_fusion
  134.6 2.8 %fusion = f32[1,2,8,256]{3,0,2,1:T(1,128)S(1)} fusion(bf16[2,8,256,256]{2,1,0,3:T(8,128)(2,1)} %bitcast.37, f32[1,256]{1,0:T(1,128)} %shard_map.59, f32[]{:T(128)S(6)} %div.41), kind=kOutput, calls=%fused_computation.1 | convolution fusion | flops 12583168 | bytes 2114564 | tf_op jit(solution)/shard_map/dot_general | solution.py:123
  137.5 0.6 copy.27
  (18 shorter events, 0.5 us)
Async XLA Ops:
  0.6 1.6 %copy-start = (bf16[8,2,256,256]{3,2,1,0:T(8,128)(2,1)S(1)}, bf16[8,2,256,256]{3,2,1,0:T(8,128)(2,1)}, u32[]{:S(2)}) copy-start(bf16[8,2,256,256]{3,2,1,0:T(8,128)(2,1)} %param.5) | copy-start | bytes 6291460
  52.9 3.5 %copy-start.1 = (bf16[256,4096]{1,0:T(8,128)(2,1)S(1)}, bf16[256,4096]{1,0:T(8,128)(2,1)}, u32[]{:S(2)}) copy-start(bf16[256,4096]{1,0:T(8,128)(2,1)} %reshape.69) | copy-start | bytes 6291460
  56.4 8.2 %copy-start.2 = (s32[8,256]{1,0:T(8,128)S(1)}, s32[8,256]{1,0:T(8,128)}, u32[]{:S(2)}) copy-start(s32[8,256]{1,0:T(8,128)} %param.4) | copy-start | bytes 24580
  56.4 8.7 %copy-start.3 = (f32[8]{0:T(128)S(1)}, f32[8]{0:T(128)}, u32[]{:S(2)}) copy-start(f32[8]{0:T(128)} %param.7) | copy-start | bytes 100
  58.7 17.2 %all-to-all-start.1 = ((f32[128,2,256]{2,1,0:T(2,128)}), f32[128,2,256]{2,1,0:T(2,128)S(1)}, u32[]{:S(2)}, u32[]{:S(2)}) async-start(f32[128,2,256]{2,1,0:T(2,128)} %reshape.70), calls=%async_computation.1 | async-start | bytes 524288 | tf_op jit(solution)/shard_map/all_to_all | solution.py:91
  76.5 10.9 %all-to-all-start.3 = ((f32[32,1,8]{2,1,0:T(1,128)}), f32[32,1,8]{2,1,0:T(1,128)S(1)}, u32[]{:S(2)}, u32[]{:S(2)}) async-start(f32[32,1,8]{2,1,0:T(1,128)} %broadcast_in_dim.9), calls=%async_computation.3 | async-start | bytes 32768 | tf_op jit(solution)/shard_map/all_to_all | solution.py:25
  88.2 15.5 %all-to-all-start.2 = ((f32[128,2,256]{2,1,0:T(2,128)}), f32[128,2,256]{2,1,0:T(2,128)S(1)}, u32[]{:S(2)}, u32[]{:S(2)}) async-start(f32[128,2,256]{2,1,0:T(2,128)} %broadcast_in_dim.7), calls=%async_computation.2 | async-start | bytes 524288 | tf_op jit(solution)/shard_map/all_to_all | solution.py:95

commit v2 on v1

v2 whole, which is shorter than its diff:
```python
import functools

import jax
import jax.numpy as jnp
from jax import lax
from jax.experimental import pallas as pl
from jax.experimental.pallas import tpu as pltpu
from jax.sharding import PartitionSpec as P

SIDE = 16
SHIFT_RATIO = 0.1
highest = lax.Precision.HIGHEST
MESH = pl.DeviceIdType.MESH
f32 = jnp.float32


def iota(shape, dim):
    return lax.broadcasted_iota(jnp.int32, shape, dim)


def local_energy(spins, offdiag_row):
    samples, sites = spins.shape
    z = (2 * spins - 1).astype(f32)
    column = iota((samples, sites), 1) % SIDE
    next_column = jnp.where(
        column == SIDE - 1,
        pltpu.roll(z, SIDE - 1, 1),
        pltpu.roll(z, sites - 1, 1),
    )
    next_row = pltpu.roll(z, sites - SIDE, 1)
    bonds = jnp.sum(z * (next_column + next_row), axis=1, keepdims=True)
    square = jnp.broadcast_to(offdiag_row, (samples, samples))
    diagonal = iota((samples, samples), 0) == iota((samples, samples), 1)
    return bonds + jnp.sum(jnp.where(diagonal, square, 0.0), axis=1, keepdims=True)


def gram_kernel(
    peers, layers,
    spins_ref, offdiag_ref, act_hbm, cot_hbm,
    rows_ref, gram_ref,
    act, cot, wide, outgoing, own_gram, pieces, sums, spread,
    in_sem, own_sem, row_send, row_recv, piece_send, piece_recv,
    sum_send, sum_recv, spread_send, spread_recv,
):
    samples, mats, sites, width = act.shape
    share = width // peers
    me = lax.axis_index("samp")
    layer = lax.axis_index("layer")

    def loads(s):
        return (
            pltpu.make_async_copy(act_hbm.at[s], act.at[s], in_sem.at[0, s]),
            pltpu.make_async_copy(cot_hbm.at[s], cot.at[s], in_sem.at[1, s]),
        )

    for s in range(samples):
        for load in loads(s):
            load.start()

    barrier = pltpu.get_barrier_semaphore()

    def greet(i, carry):
        pl.semaphore_signal(
            barrier, inc=1, device_id={"samp": lax.rem(me + i, peers)}, device_id_type=MESH
        )
        return carry

    lax.fori_loop(1, peers, greet, 0)
    for i in range(1, layers):
        pl.semaphore_signal(
            barrier, inc=1, device_id={"layer": lax.rem(layer + i, layers)}, device_id_type=MESH
        )

    energy = local_energy(spins_ref[...], offdiag_ref[...])

    def row_copy(m, peer):
        return pltpu.make_async_remote_copy(
            src_ref=outgoing.at[m, peer],
            dst_ref=rows_ref.at[m, :, me],
            send_sem=row_send.at[m],
            recv_sem=row_recv.at[m],
            device_id={"samp": peer},
            device_id_type=MESH,
        )

    for m in range(mats):
        for s in range(samples):
            if m == 0:
                for load in loads(s):
                    load.wait()
            jac = lax.dot_general(
                act[s, m], cot[s, m], (((0,), (0,)), ((), ())), preferred_element_type=f32
            )
            for h in range(width // 128):
                wide[pl.ds(h * width * samples + s, width, stride=samples), :] = jac[:, h * 128 : (h + 1) * 128]
        for h in range(width // 128):
            for k in range(peers):
                start = h * width * samples + k * share * samples
                block = wide[start : start + share * samples, :]
                outgoing[m, k, :, :, h * 128 : (h + 1) * 128] = block.reshape(share, samples, 128).astype(jnp.bfloat16)
        if m == 0:
            pl.semaphore_wait(barrier, peers + layers - 2)

        def send(i, carry):
            row_copy(m, lax.rem(me + i, peers)).start()
            return carry

        lax.fori_loop(1, peers, send, 0)
        pltpu.make_async_copy(outgoing.at[m, me], rows_ref.at[m, :, me], own_sem.at[m]).start()

    for m in range(mats):
        pltpu.make_async_copy(outgoing.at[m, me], rows_ref.at[m, :, me], own_sem.at[m]).wait()
        many = rows_ref.at[m, :, 0 : peers - 1]
        pltpu.make_async_copy(many, many, row_recv.at[m]).wait()
        total = None
        for r in range(share):
            rows = rows_ref[m, r].reshape(peers * samples, width)
            term = lax.dot_general(
                rows, rows, (((1,), (1,)), ((), ())), preferred_element_type=f32
            )
            total = term if total is None else total + term
        if m == 0:
            own_gram[...] = total
        else:
            own_gram[...] = own_gram[...] + total

    def piece_copy(peer):
        return pltpu.make_async_remote_copy(
            src_ref=own_gram.at[pl.ds(pl.multiple_of(peer * samples, samples), samples)],
            dst_ref=pieces.at[me],
            send_sem=piece_send,
            recv_sem=piece_recv,
            device_id={"samp": peer},
            device_id_type=MESH,
        )

    def send_piece(i, carry):
        piece_copy(lax.rem(me + i, peers)).start()
        return carry

    lax.fori_loop(1, peers, send_piece, 0)
    pieces[me] = own_gram[pl.ds(pl.multiple_of(me * samples, samples), samples)]
    many = pieces.at[0 : peers - 1]
    pltpu.make_async_copy(many, many, piece_recv).wait()
    sums[layer] = jnp.sum(pieces[...], axis=0)

    def sum_copy(i):
        return pltpu.make_async_remote_copy(
            src_ref=sums.at[layer],
            dst_ref=sums.at[layer],
            send_sem=sum_send.at[i],
            recv_sem=sum_recv.at[i],
            device_id={"layer": lax.rem(layer + i, layers)},
            device_id_type=MESH,
        )

    for i in range(1, layers):
        sum_copy(i).start()
    for i in range(1, layers):
        sum_copy(i).wait_recv()
    spread[:, 0:256] = jnp.sum(sums[...], axis=0)
    spread[:, 256:384] = jnp.broadcast_to(energy, (samples, 128))

    mine = pl.ds(pl.multiple_of(me * samples, samples), samples)

    def spread_copy(peer):
        return pltpu.make_async_remote_copy(
            src_ref=spread,
            dst_ref=gram_ref.at[mine],
            send_sem=spread_send,
            recv_sem=spread_recv,
            device_id={"samp": peer},
            device_id_type=MESH,
        )

    def send_spread(i, carry):
        spread_copy(lax.rem(me + i, peers)).start()
        return carry

    lax.fori_loop(1, peers, send_spread, 0)
    gram_ref[mine] = spread[...]
    for m in range(mats):
        many = outgoing.at[m, 0 : peers - 1]
        pltpu.make_async_copy(many, many, row_send.at[m]).wait()
    many = own_gram.at[0 : (peers - 1) * samples]
    pltpu.make_async_copy(many, many, piece_send).wait()
    for i in range(1, layers):
        sum_copy(i).wait_send()
    many = gram_ref.at[0 : (peers - 1) * samples]
    pltpu.make_async_copy(many, many, spread_recv).wait()
    pltpu.make_async_copy(many, many, spread_send).wait()


def gram_and_rows(spins, activations, cotangents, offdiag):
    samples, mats, sites, width = activations.shape
    peers, layers = lax.axis_size("samp"), lax.axis_size("layer")
    total, share = peers * samples, width // peers
    bf16 = jnp.bfloat16
    vmem = pl.BlockSpec(memory_space=pltpu.VMEM)
    dma = pltpu.SemaphoreType.DMA
    return pl.pallas_call(
        functools.partial(gram_kernel, peers, layers),
        out_shape=(
            jax.ShapeDtypeStruct((mats, share, peers, samples, width), bf16),
            jax.ShapeDtypeStruct((total, total + 128), f32),
        ),
        in_specs=[vmem, vmem, pl.BlockSpec(memory_space=pl.ANY), pl.BlockSpec(memory_space=pl.ANY)],
        out_specs=(vmem, vmem),
        scratch_shapes=[
            pltpu.VMEM(activations.shape, bf16),
            pltpu.VMEM(cotangents.shape, bf16),
            pltpu.VMEM((width // 128 * width * samples, 128), f32),
            pltpu.VMEM((mats, peers, share, samples, width), bf16),
            pltpu.VMEM((total, total), f32),
            pltpu.VMEM((peers, samples, total), f32),
            pltpu.VMEM((layers, samples, total), f32),
            pltpu.VMEM((samples, total + 128), f32),
            dma((2, samples)),
            dma((mats,)),
            dma((mats,)),
            dma((mats,)),
            dma,
            dma,
            dma((layers,)),
            dma((layers,)),
            dma,
            dma,
        ],
        compiler_params=pltpu.CompilerParams(
            collective_id=0, has_side_effects=True, vmem_limit_bytes=48 << 20
        ),
    )(spins, offdiag[None, :], activations, cotangents)


def tile_inverse(tile):
    order = tile.shape[0]
    sub, lane = iota((order, order), 0), iota((order, order), 1)
    sub_col, lane_row = iota((order, 1), 0), iota((1, order), 1)
    for k in range(order):
        row = tile[k : k + 1, :]
        col = tile[:, k : k + 1]
        inv_pivot = 1.0 / tile[k : k + 1, k : k + 1]
        scaled = jnp.where(lane_row == k, 1.0, row) * inv_pivot
        kept = jnp.where((lane == k) | (sub == k), 0.0, tile)
        tile = kept - jnp.where(sub_col == k, -1.0, col) * scaled
    return tile


def solve_kernel(block, rows_ref, gram_ref, weights_ref, update_ref, work):
    mats, share, peers, samples, width = rows_ref.shape
    total = peers * samples
    me = lax.axis_index("samp")
    raw = gram_ref[:, 0:total]
    means = jnp.mean(raw, axis=1, keepdims=True)
    diagonal = iota((total, total), 0) == iota((total, total), 1)

    def as_row(col):
        return jnp.sum(jnp.where(diagonal, col, 0.0), axis=0, keepdims=True)

    means_row = as_row(means)
    gram = (raw - means - means_row + jnp.mean(means_row)) / total
    trace = jnp.sum(jnp.where(diagonal, gram, 0.0))
    work[0:total, :] = gram + jnp.where(diagonal, SHIFT_RATIO * trace / total, 0.0)
    energy = as_row(gram_ref[:, total : total + 1])
    eps = (energy - jnp.mean(energy)) / jnp.sqrt(f32(total))
    work[total : total + 8, :] = jnp.broadcast_to(eps, (8, total))
    lane = iota((1, total), 1)
    for k in range(total // block):
        own = slice(k * block, (k + 1) * block)
        below = slice((k + 1) * block, total + 8)
        inverse = tile_inverse(work[own, own])
        scaled = jnp.dot(work[below, own], inverse, precision=highest, preferred_element_type=f32)
        inside = (lane >= k * block) & (lane < (k + 1) * block)
        pivot_rows = jnp.where(inside, 0.0, work[own, :])
        work[below, :] = work[below, :] - jnp.dot(
            scaled, pivot_rows, precision=highest, preferred_element_type=f32
        )
        work[below, own] = scaled
    weights = work[total : total + 1, :]
    weights_ref[...] = pltpu.roll(weights, total - me * samples, 1)[:, 0:samples]
    coeffs = weights - jnp.mean(weights)
    first = coeffs.astype(jnp.bfloat16)
    rest = coeffs - first.astype(f32)
    second = rest.astype(jnp.bfloat16)
    third = (rest - second.astype(f32)).astype(jnp.bfloat16)
    split = jnp.concatenate(
        [first.astype(f32), second.astype(f32), third.astype(f32), jnp.zeros((5, total), f32)], axis=0
    ).astype(jnp.bfloat16)
    for m in range(mats):
        for r in range(share):
            rows = rows_ref[m, r].reshape(total, width)
            parts = jnp.dot(split, rows, preferred_element_type=f32)
            update_ref[m, r : r + 1, :] = jnp.sum(parts, axis=0, keepdims=True)


def solve_and_update(rows, gram):
    mats, share, peers, samples, width = rows.shape
    total = peers * samples
    vmem = pl.BlockSpec(memory_space=pltpu.VMEM)
    return pl.pallas_call(
        functools.partial(solve_kernel, 64),
        out_shape=(
            jax.ShapeDtypeStruct((1, samples), f32),
            jax.ShapeDtypeStruct((mats, share, width), f32),
        ),
        in_specs=[vmem, vmem],
        out_specs=(vmem, vmem),
        scratch_shapes=[pltpu.VMEM((total + 8, total), f32)],
    )(rows, gram)


def body(spins, activations, cotangents, offdiag):
    rows, gram = gram_and_rows(spins, activations, cotangents, offdiag)
    weights, update = solve_and_update(rows, gram)
    return weights[0], update


def solution(mesh):
    placed = (
        P("samp", None),
        P("samp", "layer", None, None),
        P("samp", "layer", None, None),
        P("samp"),
    )
    return jax.shard_map(
        body,
        mesh=mesh,
        in_specs=placed,
        out_specs=(P("samp"), P("layer", "samp", None)),
        check_vma=False,
    )
```

time: 139 us -> 90.3 us (0.65)
  Pallas kernels: 25.2 us -> 84.4 us
  blocking collectives: 37.6 us -> 0 us
  waiting for transfers between devices: 23.3 us -> 0 us
  local copies, waits for them, and re-layouts: 19.4 us -> 5.03 us
  starting transfers between devices: 14.1 us -> 0 us
  matrix products: 10.1 us -> 0 us
  other arithmetic: 5.83 us -> 0 us
  between operations: 2.76 us -> 0.66 us
    pallas_call x1 -> x2, Pallas kernels: 25.2 us -> 84.4 us  [the longest x1 57.5 us: gram_and_rows(): pl.pallas_call(functools.partial(gram_kernel, peers, layers), out_shape=(...]
    all_to_all x1 -> x0, blocking collectives: 37.6 us -> none  [body(): lax.all_to_all(jac, 'samp', split_axis=2, concat_axis=0, tiled=True)]
    all_to_all x3 -> x0, waiting for transfers between devices: 23.3 us -> none  [the longest x1 10.8 us: sum_directly(): lax.all_to_all(partial_sum.reshape(devices, rows, -1), axes, 0, 0, tiled=...]
    all_to_all x3 -> x0, starting transfers between devices: 14.1 us -> none  [the longest x1 5.85 us: sum_directly(): lax.all_to_all(partial_sum.reshape(devices, rows, -1), axes, 0, 0, tiled=...]
    dot_general x4 -> x0, matrix products: 10.1 us -> none  [the longest x1 3.46 us: body(): row_dots = jnp.dot(flat.astype(jnp.float32), col_mean, precision=highest)]
    reshape x4 -> x0, local copies, waits for them, and re-layouts: 5.33 us -> none  [the longest x1 4.2 us: body(): flat = regrouped.reshape(total, -1)]
    reduce_sum x6 -> x0, other arithmetic: 4.34 us -> none  [the longest x1 1.27 us: body(): coeffs_all = weights - jnp.mean(weights)]
    all_to_all x1 -> x0, local copies, waits for them, and re-layouts: 2.62 us -> none  [body(): lax.all_to_all(jac, 'samp', split_axis=2, concat_axis=0, tiled=True)]
  transfers between devices with their start and end apart: 3 -> 0, of which waited for: 3 -> 0; matrix products, arithmetic and copies ran while one was open for 4% -> 0% of each run, Pallas kernels for 0% -> 0%
where the time goes in v2:
time: 90.3 us; the launch traced here: 90.1 us
  Pallas kernels  84.4 us (93%)
  local copies, waits for them, and re-layouts  5.03 us (6%)
    pallas_call x1, Pallas kernels, gram_and_rows(): pl.pallas_call(functools.partial(gram_kernel, peers, layers), out_shape=(...  57.5 us
    pallas_call x1, Pallas kernels, solve_and_update(): pl.pallas_call(functools.partial(solve_kernel, 64), out_shape=(jax.ShapeD...  26.9 us
    unnamed x10, local copies, waits for them, and re-layouts  5.03 us

profile of v2, /device:TPU:1, one launch (start us, length us, event | category | flops | bytes accessed | tf_op | source)
XLA Modules:
  0.0 90.1 jit_solution(10806748362290943499)
XLA Ops:
  0.6 0.0 copy-start.1
  0.6 1.6 %copy-done.1 = bf16[8,2,256,256]{3,2,1,0:T(8,128)(2,1)S(1)} copy-done((bf16[8,2,256,256]{3,2,1,0:T(8,128)(2,1)S(1)}, bf16[8,2,256,256]{3,2,1,0:T(8,128)(2,1)}, u32[]{:S(2)}) %copy-start.1) | copy-done | bytes 2097176
  2.2 0.0 copy-start.3
  2.2 0.7 copy-done.3
  2.9 0.0 copy-start.4
  2.9 0.7 copy-done.4
  3.6 57.5 %shard_map.59 = (bf16[2,8,32,8,256]{4,3,2,1,0:T(8,128)(2,1)S(1)}, f32[256,384]{1,0:T(8,128)S(1)}) custom-call(s32[8,256]{1,0:T(8,128)S(1)} %copy-done.3, f32[1,8]{1,0:T(1,128)S(1)} %bitcast.2, bf16[8,2,256,256]{3,2,1,0:T(8,128)(2,1)S(1)} %copy-done.1, bf16[8,2,256,256]{3,2,1,0:T(8,128)(2,1)} %cot_hbm.1), custom_call_target="tpu_custom_call" | custom-call | tf_op jit(solution)/shard_map/pallas_call | solution.py:201
  61.1 0.0 copy-start
  61.1 1.3 %copy-done = bf16[2,8,32,8,256]{4,3,2,1,0:T(8,128)(2,1)} copy-done((bf16[2,8,32,8,256]{4,3,2,1,0:T(8,128)(2,1)}, bf16[2,8,32,8,256]{4,3,2,1,0:T(8,128)(2,1)S(1)}, u32[]{:S(2)}) %copy-start) | copy-done | bytes 2097176
  62.5 0.0 copy-start.2
  62.5 0.7 copy-done.2
  63.2 26.9 %shard_map.60 = (f32[1,8]{1,0:T(1,128)}, f32[2,8,256]{2,1,0:T(8,128)}) custom-call(bf16[2,8,32,8,256]{4,3,2,1,0:T(8,128)(2,1)} %copy-done, f32[256,384]{1,0:T(8,128)} %copy-done.2), custom_call_target="tpu_custom_call" | custom-call | tf_op jit(solution)/shard_map/pallas_call | solution.py:300
Async XLA Ops:
  0.6 1.6 %copy-start.1 = (bf16[8,2,256,256]{3,2,1,0:T(8,128)(2,1)S(1)}, bf16[8,2,256,256]{3,2,1,0:T(8,128)(2,1)}, u32[]{:S(2)}) copy-start(bf16[8,2,256,256]{3,2,1,0:T(8,128)(2,1)} %act_hbm.1) | copy-start | bytes 6291460
  2.2 0.7 copy-start.3
  2.9 0.7 copy-start.4
  61.1 1.4 %copy-start = (bf16[2,8,32,8,256]{4,3,2,1,0:T(8,128)(2,1)}, bf16[2,8,32,8,256]{4,3,2,1,0:T(8,128)(2,1)S(1)}, u32[]{:S(2)}) copy-start(bf16[2,8,32,8,256]{4,3,2,1,0:T(8,128)(2,1)S(1)} %get-tuple-element.6.rows_ref) | copy-start | bytes 6291460
  62.5 0.8 copy-start.2

commit v3 on v2

--- a/solution.py
+++ b/solution.py
@@ -12,6 +12,14 @@
 highest = lax.Precision.HIGHEST
 MESH = pl.DeviceIdType.MESH
 f32 = jnp.float32
+CHIPS = (2, 2), (2, 1), (1, 2), (2, 3), (3, 2), (1, 1), (3, 3), (1, 3), (3, 1), (2, 0), (0, 2), (1, 0), (3, 0), (0, 1), (0, 3)
+FAR_FIRST = [(y, z, c) for c in (0, 1) for y, z in CHIPS] + [(0, 0, 1)]
+
+
+def peer_at(me, step):
+    y, z, core = step
+    row, col = me // 8, me // 2 % 4
+    return (row + y) % 4 * 8 + (col + z) % 4 * 2 + (me + core) % 2
 
 
 def iota(shape, dim):
@@ -31,14 +39,17 @@
     bonds = jnp.sum(z * (next_column + next_row), axis=1, keepdims=True)
     square = jnp.broadcast_to(offdiag_row, (samples, samples))
     diagonal = iota((samples, samples), 0) == iota((samples, samples), 1)
-    return bonds + jnp.sum(jnp.where(diagonal, square, 0.0), axis=1, keepdims=True)
+    energy = bonds + jnp.sum(jnp.where(diagonal, square, 0.0), axis=1, keepdims=True)
+    repeated = iota((samples, sites), 1) % samples == iota((samples, sites), 0)
+    return jnp.sum(jnp.where(repeated, energy, 0.0), axis=0, keepdims=True)
 
 
 def gram_kernel(
     peers, layers,
-    spins_ref, offdiag_ref, act_hbm, cot_hbm,
-    rows_ref, gram_ref,
-    act, cot, wide, outgoing, own_gram, pieces, sums, spread,
+    spins_hbm, offdiag_hbm, act_hbm, cot_hbm,
+    rows_ref, gram_ref, energy_ref,
+    spins, offdiag, act, cot, wide, outgoing, own_gram, pieces, sums, spread, energy,
+    small_sem, energy_send, energy_recv,
     in_sem, own_sem, row_send, row_recv, piece_send, piece_recv,
     sum_send, sum_recv, spread_send, spread_recv,
 ):
@@ -53,6 +64,12 @@
             pltpu.make_async_copy(cot_hbm.at[s], cot.at[s], in_sem.at[1, s]),
         )
 
+    small = (
+        pltpu.make_async_copy(spins_hbm, spins, small_sem.at[0]),
+        pltpu.make_async_copy(offdiag_hbm, offdiag, small_sem.at[1]),
+    )
+    for load in small:
+        load.start()
     for s in range(samples):
         for load in loads(s):
             load.start()
@@ -71,7 +88,20 @@
             barrier, inc=1, device_id={"layer": lax.rem(layer + i, layers)}, device_id_type=MESH
         )
 
-    energy = local_energy(spins_ref[...], offdiag_ref[...])
+    for load in small:
+        load.wait()
+    energy[...] = local_energy(spins[...], offdiag[...])
+    steps = [peer_at(me, step) for step in FAR_FIRST]
+
+    def energy_copy(peer):
+        return pltpu.make_async_remote_copy(
+            src_ref=energy,
+            dst_ref=energy_ref.at[me],
+            send_sem=energy_send,
+            recv_sem=energy_recv,
+            device_id={"samp": peer},
+            device_id_type=MESH,
+        )
 
     def row_copy(m, peer):
         return pltpu.make_async_remote_copy(
@@ -100,12 +130,12 @@
                 outgoing[m, k, :, :, h * 128 : (h + 1) * 128] = block.reshape(share, samples, 128).astype(jnp.bfloat16)
         if m == 0:
             pl.semaphore_wait(barrier, peers + layers - 2)
-
-        def send(i, carry):
-            row_copy(m, lax.rem(me + i, peers)).start()
-            return carry
-
-        lax.fori_loop(1, peers, send, 0)
+        for peer in steps:
+            row_copy(m, peer).start()
+        if m == 0:
+            for peer in steps:
+                energy_copy(peer).start()
+            energy_ref[me] = energy[...]
         pltpu.make_async_copy(outgoing.at[m, me], rows_ref.at[m, :, me], own_sem.at[m]).start()
 
     for m in range(mats):
@@ -134,11 +164,8 @@
             device_id_type=MESH,
         )
 
-    def send_piece(i, carry):
-        piece_copy(lax.rem(me + i, peers)).start()
-        return carry
-
-    lax.fori_loop(1, peers, send_piece, 0)
+    for peer in steps:
+        piece_copy(peer).start()
     pieces[me] = own_gram[pl.ds(pl.multiple_of(me * samples, samples), samples)]
     many = pieces.at[0 : peers - 1]
     pltpu.make_async_copy(many, many, piece_recv).wait()
@@ -154,12 +181,11 @@
             device_id_type=MESH,
         )
 
-    for i in range(1, layers):
+    for i in (2, 1, 3):
         sum_copy(i).start()
     for i in range(1, layers):
         sum_copy(i).wait_recv()
-    spread[:, 0:256] = jnp.sum(sums[...], axis=0)
-    spread[:, 256:384] = jnp.broadcast_to(energy, (samples, 128))
+    spread[...] = jnp.sum(sums[...], axis=0)
 
     mine = pl.ds(pl.multiple_of(me * samples, samples), samples)
 
@@ -173,15 +199,15 @@
             device_id_type=MESH,
         )
 
-    def send_spread(i, carry):
-        spread_copy(lax.rem(me + i, peers)).start()
-        return carry
-
-    lax.fori_loop(1, peers, send_spread, 0)
+    for peer in steps:
+        spread_copy(peer).start()
     gram_ref[mine] = spread[...]
     for m in range(mats):
         many = outgoing.at[m, 0 : peers - 1]
         pltpu.make_async_copy(many, many, row_send.at[m]).wait()
+    many = energy_ref.at[0 : peers - 1]
+    pltpu.make_async_copy(many, many, energy_send).wait()
+    pltpu.make_async_copy(many, many, energy_recv).wait()
     many = own_gram.at[0 : (peers - 1) * samples]
     pltpu.make_async_copy(many, many, piece_send).wait()
     for i in range(1, layers):
@@ -202,11 +228,14 @@
         functools.partial(gram_kernel, peers, layers),
         out_shape=(
             jax.ShapeDtypeStruct((mats, share, peers, samples, width), bf16),
-            jax.ShapeDtypeStruct((total, total + 128), f32),
+            jax.ShapeDtypeStruct((total, total), f32),
+            jax.ShapeDtypeStruct((peers, 1, total), f32),
         ),
-        in_specs=[vmem, vmem, pl.BlockSpec(memory_space=pl.ANY), pl.BlockSpec(memory_space=pl.ANY)],
-        out_specs=(vmem, vmem),
+        in_specs=[pl.BlockSpec(memory_space=pltpu.HBM)] * 4,
+        out_specs=(vmem, vmem, vmem),
         scratch_shapes=[
+            pltpu.VMEM(spins.shape, jnp.int32),
+            pltpu.VMEM((1, samples), f32),
             pltpu.VMEM(activations.shape, bf16),
             pltpu.VMEM(cotangents.shape, bf16),
             pltpu.VMEM((width // 128 * width * samples, 128), f32),
@@ -214,7 +243,11 @@
             pltpu.VMEM((total, total), f32),
             pltpu.VMEM((peers, samples, total), f32),
             pltpu.VMEM((layers, samples, total), f32),
-            pltpu.VMEM((samples, total + 128), f32),
+            pltpu.VMEM((samples, total), f32),
+            pltpu.VMEM((1, total), f32),
+            dma((2,)),
+            dma,
+            dma,
             dma((2, samples)),
             dma((mats,)),
             dma((mats,)),
@@ -227,9 +260,9 @@
             dma,
         ],
         compiler_params=pltpu.CompilerParams(
-            collective_id=0, has_side_effects=True, vmem_limit_bytes=48 << 20
+            collective_id=0, has_side_effects=True, vmem_limit_bytes=20 << 20
         ),
-    )(spins, offdiag[None, :], activations, cotangents)
+    )(*(pltpu.with_memory_space_constraint(a, pltpu.HBM) for a in (spins, offdiag[None, :], activations, cotangents)))
 
 
 def tile_inverse(tile):
@@ -246,11 +279,11 @@
     return tile
 
 
-def solve_kernel(block, rows_ref, gram_ref, weights_ref, update_ref, work):
+def solve_kernel(block, rows_ref, gram_ref, energy_ref, weights_ref, update_ref, work):
     mats, share, peers, samples, width = rows_ref.shape
     total = peers * samples
     me = lax.axis_index("samp")
-    raw = gram_ref[:, 0:total]
+    raw = gram_ref[...]
     means = jnp.mean(raw, axis=1, keepdims=True)
     diagonal = iota((total, total), 0) == iota((total, total), 1)
 
@@ -261,7 +294,9 @@
     gram = (raw - means - means_row + jnp.mean(means_row)) / total
     trace = jnp.sum(jnp.where(diagonal, gram, 0.0))
     work[0:total, :] = gram + jnp.where(diagonal, SHIFT_RATIO * trace / total, 0.0)
-    energy = as_row(gram_ref[:, total : total + 1])
+    every = energy_ref[...].reshape(peers, total)
+    held = iota((peers, total), 1) // samples == iota((peers, total), 0)
+    energy = jnp.sum(jnp.where(held, every, 0.0), axis=0, keepdims=True)
     eps = (energy - jnp.mean(energy)) / jnp.sqrt(f32(total))
     work[total : total + 8, :] = jnp.broadcast_to(eps, (8, total))
     lane = iota((1, total), 1)
@@ -293,7 +328,7 @@
             update_ref[m, r : r + 1, :] = jnp.sum(parts, axis=0, keepdims=True)
 
 
-def solve_and_update(rows, gram):
+def solve_and_update(rows, gram, energy):
     mats, share, peers, samples, width = rows.shape
     total = peers * samples
     vmem = pl.BlockSpec(memory_space=pltpu.VMEM)
@@ -303,15 +338,16 @@
             jax.ShapeDtypeStruct((1, samples), f32),
             jax.ShapeDtypeStruct((mats, share, width), f32),
         ),
-        in_specs=[vmem, vmem],
+        in_specs=[vmem, vmem, vmem],
         out_specs=(vmem, vmem),
         scratch_shapes=[pltpu.VMEM((total + 8, total), f32)],
-    )(rows, gram)
+        compiler_params=pltpu.CompilerParams(vmem_limit_bytes=20 << 20),
+    )(rows, gram, energy)
 
 
 def body(spins, activations, cotangents, offdiag):
-    rows, gram = gram_and_rows(spins, activations, cotangents, offdiag)
-    weights, update = solve_and_update(rows, gram)
+    rows, gram, energy = gram_and_rows(spins, activations, cotangents, offdiag)
+    weights, update = solve_and_update(rows, gram, energy)
     return weights[0], update
 
 

time: 90.3 us -> 76.3 us (0.84)
  Pallas kernels: 84.4 us -> 75.6 us
  local copies, waits for them, and re-layouts: 5.03 us -> 0 us
    pallas_call x1, Pallas kernels: 57.5 us -> 50.3 us  [gram_and_rows(): pl.pallas_call(functools.partial(gram_kernel, peers, layers), out_shape=(...]
    unnamed x10 -> x0, local copies, waits for them, and re-layouts: 5.03 us -> none
    pallas_call x1, Pallas kernels: 26.9 us -> 25.2 us  [solve_and_update(): pl.pallas_call(functools.partial(solve_kernel, 64), out_shape=(jax.ShapeD...]
where the time goes in v3:
time: 76.3 us; the launch traced here: 76.2 us
  Pallas kernels  75.6 us (99%)
    pallas_call x1, Pallas kernels, gram_and_rows(): pl.pallas_call(functools.partial(gram_kernel, peers, layers), out_shape=(...  50.3 us
    pallas_call x1, Pallas kernels, solve_and_update(): pl.pallas_call(functools.partial(solve_kernel, 64), out_shape=(jax.ShapeD...  25.2 us

profile of v3, /device:TPU:1, one launch (start us, length us, event | category | flops | bytes accessed | tf_op | source)
XLA Modules:
  0.0 76.2 jit_solution(12650057712204597387)
XLA Ops:
  0.6 50.3 %shard_map.59 = (bf16[2,8,32,8,256]{4,3,2,1,0:T(8,128)(2,1)S(1)}, f32[256,256]{1,0:T(8,128)S(1)}, f32[32,1,256]{2,1,0:T(1,128)S(1)}) custom-call(s32[8,256]{1,0:T(8,128)} %spins_hbm.1, f32[1,8]{1,0:T(1,128)} %bitcast.2, bf16[8,2,256,256]{3,2,1,0:T(8,128)(2,1)} %act_hbm.1, bf16[8,2,256,256]{3,2,1,0:T(8,128)(2,1)} %cot_hbm.1), custom_call_target="tpu_custom_call" | custom-call | tf_op jit(solution)/shard_map/pallas_call | solution.py:227
  51.0 25.2 %shard_map.60 = (f32[1,8]{1,0:T(1,128)}, f32[2,8,256]{2,1,0:T(8,128)}) custom-call(bf16[2,8,32,8,256]{4,3,2,1,0:T(8,128)(2,1)S(1)} %get-tuple-element.7.rows_ref, f32[256,256]{1,0:T(8,128)S(1)} %get-tuple-element.8.gram_ref, f32[32,1,256]{2,1,0:T(1,128)S(1)} %get-tuple-element.9.energy_ref), custom_call_target="tpu_custom_call" | custom-call | tf_op jit(solution)/shard_map/pallas_call | solution.py:335

commit v4 on v3

--- a/solution.py
+++ b/solution.py
@@ -265,21 +265,94 @@
     )(*(pltpu.with_memory_space_constraint(a, pltpu.HBM) for a in (spins, offdiag[None, :], activations, cotangents)))
 
 
-def tile_inverse(tile):
-    order = tile.shape[0]
-    sub, lane = iota((order, order), 0), iota((order, order), 1)
-    sub_col, lane_row = iota((order, 1), 0), iota((1, order), 1)
-    for k in range(order):
-        row = tile[k : k + 1, :]
-        col = tile[:, k : k + 1]
-        inv_pivot = 1.0 / tile[k : k + 1, k : k + 1]
-        scaled = jnp.where(lane_row == k, 1.0, row) * inv_pivot
-        kept = jnp.where((lane == k) | (sub == k), 0.0, tile)
-        tile = kept - jnp.where(sub_col == k, -1.0, col) * scaled
-    return tile
-
-
-def solve_kernel(block, rows_ref, gram_ref, energy_ref, weights_ref, update_ref, work):
+def minus_inverse(entry, order):
+    at = lambda i, j: entry[min(i, j), max(i, j)]
+    for p in range(0, order, 2):
+        q = p + 1
+        first, cross, second = entry[p, p], entry[p, q], entry[q, q]
+        scale = 1.0 / (first * second - cross * cross)
+        inv_pp, inv_pq, inv_qq = second * scale, cross * scale, first * scale
+        others = [i for i in range(order) if i not in (p, q)]
+        gain = {
+            i: (
+                at(i, p) * inv_pp - at(i, q) * inv_pq,
+                at(i, q) * inv_qq - at(i, p) * inv_pq,
+            )
+            for i in others
+        }
+        fresh = {}
+        for x, i in enumerate(others):
+            for j in others[x:]:
+                fresh[i, j] = entry[i, j] - (gain[i][0] * at(j, p) + gain[i][1] * at(j, q))
+            fresh[min(i, p), max(i, p)] = gain[i][0]
+            fresh[min(i, q), max(i, q)] = gain[i][1]
+        fresh[p, p], fresh[p, q], fresh[q, q] = -inv_pp, inv_pq, -inv_qq
+        entry = fresh
+        at = lambda i, j, entry=entry: entry[min(i, j), max(i, j)]
+    return entry
+
+
+def tree_sum(terms):
+    while len(terms) > 1:
+        terms = [a + b for a, b in zip(terms[::2], terms[1::2], strict=True)]
+    return terms[0]
+
+
+def sweep(groups, k):
+    shape = groups[k].shape
+    lane, sub = iota(shape, 1), iota(shape, 0)
+    start = 8 * k
+    pivot_rows = [jnp.broadcast_to(groups[k][i : i + 1, :], shape) for i in range(8)]
+    entry = {
+        (i, j): jnp.broadcast_to(pivot_rows[i][:, start + j : start + j + 1], shape)
+        for i in range(8)
+        for j in range(i, 8)
+    }
+    entry = minus_inverse(entry, 8)
+    inside = (lane >= start) & (lane < start + 8)
+    marked = [
+        jnp.where(inside, jnp.where(lane == start + j, -1.0, 0.0), pivot_rows[j]) for j in range(8)
+    ]
+    scaled = [
+        tree_sum([entry[min(i, j), max(i, j)] * marked[j] for j in range(8)]) for i in range(8)
+    ]
+    swept = []
+    for v, group in enumerate(groups):
+        if v == k:
+            fresh = -scaled[7]
+            for i in range(7):
+                fresh = jnp.where(sub == i, -scaled[i], fresh)
+        else:
+            fresh = jnp.where(inside, 0.0, group) + tree_sum(
+                [jnp.broadcast_to(group[:, start + i : start + i + 1], shape) * scaled[i] for i in range(8)]
+            )
+        swept.append(fresh)
+    return swept
+
+
+def solve(matrix, inverse, rhs):
+    half = matrix.shape[0] // 2
+    dot = functools.partial(jnp.dot, precision=highest, preferred_element_type=f32)
+    count = half // 8
+    groups = [matrix[8 * v : 8 * v + 8, 0:half] for v in range(count)]
+    groups.append(jnp.broadcast_to(rhs[:, 0:half], (8, half)))
+    for k in range(count):
+        groups = sweep(groups, k)
+    for v in range(count):
+        inverse[8 * v : 8 * v + 8, :] = groups[v]
+    top = groups[count]
+    cross = -dot(matrix[half : 2 * half, 0:half], inverse[...])
+    rest = matrix[half : 2 * half, half : 2 * half] - dot(cross, matrix[0:half, half : 2 * half])
+    groups = [rest[8 * v : 8 * v + 8, :] for v in range(count)]
+    groups.append(rhs[:, half : 2 * half] - dot(top, matrix[0:half, half : 2 * half]))
+    for k in range(count):
+        groups = sweep(groups, k)
+    bottom = groups[count]
+    top = top - dot(bottom, cross)
+    return jnp.concatenate([top[0:1, :], bottom[0:1, :]], axis=1)
+
+
+def solve_kernel(rows_ref, gram_ref, energy_ref, weights_ref, update_ref, work, inverse):
     mats, share, peers, samples, width = rows_ref.shape
     total = peers * samples
     me = lax.axis_index("samp")
@@ -293,25 +366,12 @@
     means_row = as_row(means)
     gram = (raw - means - means_row + jnp.mean(means_row)) / total
     trace = jnp.sum(jnp.where(diagonal, gram, 0.0))
-    work[0:total, :] = gram + jnp.where(diagonal, SHIFT_RATIO * trace / total, 0.0)
+    work[...] = gram + jnp.where(diagonal, SHIFT_RATIO * trace / total, 0.0)
     every = energy_ref[...].reshape(peers, total)
     held = iota((peers, total), 1) // samples == iota((peers, total), 0)
     energy = jnp.sum(jnp.where(held, every, 0.0), axis=0, keepdims=True)
     eps = (energy - jnp.mean(energy)) / jnp.sqrt(f32(total))
-    work[total : total + 8, :] = jnp.broadcast_to(eps, (8, total))
-    lane = iota((1, total), 1)
-    for k in range(total // block):
-        own = slice(k * block, (k + 1) * block)
-        below = slice((k + 1) * block, total + 8)
-        inverse = tile_inverse(work[own, own])
-        scaled = jnp.dot(work[below, own], inverse, precision=highest, preferred_element_type=f32)
-        inside = (lane >= k * block) & (lane < (k + 1) * block)
-        pivot_rows = jnp.where(inside, 0.0, work[own, :])
-        work[below, :] = work[below, :] - jnp.dot(
-            scaled, pivot_rows, precision=highest, preferred_element_type=f32
-        )
-        work[below, own] = scaled
-    weights = work[total : total + 1, :]
+    weights = solve(work, inverse, eps)
     weights_ref[...] = pltpu.roll(weights, total - me * samples, 1)[:, 0:samples]
     coeffs = weights - jnp.mean(weights)
     first = coeffs.astype(jnp.bfloat16)
@@ -333,14 +393,14 @@
     total = peers * samples
     vmem = pl.BlockSpec(memory_space=pltpu.VMEM)
     return pl.pallas_call(
-        functools.partial(solve_kernel, 64),
+        solve_kernel,
         out_shape=(
             jax.ShapeDtypeStruct((1, samples), f32),
             jax.ShapeDtypeStruct((mats, share, width), f32),
         ),
         in_specs=[vmem, vmem, vmem],
         out_specs=(vmem, vmem),
-        scratch_shapes=[pltpu.VMEM((total + 8, total), f32)],
+        scratch_shapes=[pltpu.VMEM((total, total), f32), pltpu.VMEM((total // 2, total // 2), f32)],
         compiler_params=pltpu.CompilerParams(vmem_limit_bytes=20 << 20),
     )(rows, gram, energy)
 

time: 76.3 us -> 63.5 us (0.83)
  Pallas kernels: 75.6 us -> 62.8 us
    pallas_call x1, Pallas kernels: 25.2 us -> 12.4 us  [solve_and_update(): pl.pallas_call(solve_kernel, out_shape=(jax.ShapeDtypeStruct((1, samples)...]
where the time goes in v4:
time: 63.5 us; the launch traced here: 63.4 us
  Pallas kernels  62.8 us (99%)
  between operations  0.64 us (1%)
    pallas_call x1, Pallas kernels, gram_and_rows(): pl.pallas_call(functools.partial(gram_kernel, peers, layers), out_shape=(...  50.3 us
    pallas_call x1, Pallas kernels, solve_and_update(): pl.pallas_call(solve_kernel, out_shape=(jax.ShapeDtypeStruct((1, samples)...  12.4 us

profile of v4, /device:TPU:1, one launch (start us, length us, event | category | flops | bytes accessed | tf_op | source)
XLA Modules:
  0.0 63.4 jit_solution(860842288225570165)
XLA Ops:
  0.6 50.3 %shard_map.59 = (bf16[2,8,32,8,256]{4,3,2,1,0:T(8,128)(2,1)S(1)}, f32[256,256]{1,0:T(8,128)S(1)}, f32[32,1,256]{2,1,0:T(1,128)S(1)}) custom-call(s32[8,256]{1,0:T(8,128)} %spins_hbm.1, f32[1,8]{1,0:T(1,128)} %bitcast.2, bf16[8,2,256,256]{3,2,1,0:T(8,128)(2,1)} %act_hbm.1, bf16[8,2,256,256]{3,2,1,0:T(8,128)(2,1)} %cot_hbm.1), custom_call_target="tpu_custom_call" | custom-call | tf_op jit(solution)/shard_map/pallas_call | solution.py:227
  51.0 12.4 %shard_map.60 = (f32[1,8]{1,0:T(1,128)}, f32[2,8,256]{2,1,0:T(8,128)}) custom-call(bf16[2,8,32,8,256]{4,3,2,1,0:T(8,128)(2,1)S(1)} %get-tuple-element.7.rows_ref, f32[256,256]{1,0:T(8,128)S(1)} %get-tuple-element.8.gram_ref, f32[32,1,256]{2,1,0:T(1,128)S(1)} %get-tuple-element.9.energy_ref), custom_call_target="tpu_custom_call" | custom-call | tf_op jit(solution)/shard_map/pallas_call | solution.py:395

commit v5 on v4

--- a/solution.py
+++ b/solution.py
@@ -298,61 +298,89 @@
     return terms[0]
 
 
-def sweep(groups, k):
+def spread_columns(group, start):
+    return [jnp.broadcast_to(group[:, start + j : start + j + 1], group.shape) for j in range(8)]
+
+
+def sweep(groups, k, own_columns, shelf):
     shape = groups[k].shape
     lane, sub = iota(shape, 1), iota(shape, 0)
-    start = 8 * k
-    pivot_rows = [jnp.broadcast_to(groups[k][i : i + 1, :], shape) for i in range(8)]
-    entry = {
-        (i, j): jnp.broadcast_to(pivot_rows[i][:, start + j : start + j + 1], shape)
-        for i in range(8)
-        for j in range(i, 8)
-    }
+    start, slot = 8 * k, k % 2
+
+    def put(place, tiles):
+        for j, tile in enumerate(tiles):
+            shelf[slot, place + 8 * j : place + 8 * j + 8, :] = tile
+
+    def spread_row(place, j, i):
+        return shelf[slot, pl.ds(place + 8 * j + i, 8, stride=0), :]
+
+    put(0, own_columns)
+    entry = {(i, j): spread_row(0, j, i) for i in range(8) for j in range(i, 8)}
     entry = minus_inverse(entry, 8)
+    at = lambda i, j: entry[min(i, j), max(i, j)]
+    next_columns, columns = None, {}
+    if start + 8 < shape[1]:
+        near = columns[k + 1] = spread_columns(groups[k + 1], start)
+        put(64, near)
+        gains = [tree_sum([at(i, a) * near[a] for a in range(8)]) for i in range(8)]
+        old = spread_columns(groups[k + 1], start + 8)
+        next_columns = [
+            old[j] + tree_sum([gains[i] * spread_row(64, i, j) for i in range(8)]) for j in range(8)
+        ]
+    put(128, [groups[k]])
     inside = (lane >= start) & (lane < start + 8)
     marked = [
-        jnp.where(inside, jnp.where(lane == start + j, -1.0, 0.0), pivot_rows[j]) for j in range(8)
+        jnp.where(inside, jnp.where(lane == start + j, -1.0, 0.0), spread_row(128, 0, j)) for j in range(8)
     ]
-    scaled = [
-        tree_sum([entry[min(i, j), max(i, j)] * marked[j] for j in range(8)]) for i in range(8)
-    ]
-    swept = []
-    for v, group in enumerate(groups):
-        if v == k:
-            fresh = -scaled[7]
-            for i in range(7):
-                fresh = jnp.where(sub == i, -scaled[i], fresh)
-        else:
-            fresh = jnp.where(inside, 0.0, group) + tree_sum(
-                [jnp.broadcast_to(group[:, start + i : start + i + 1], shape) * scaled[i] for i in range(8)]
-            )
-        swept.append(fresh)
-    return swept
-
-
-def solve(matrix, inverse, rhs):
+    scaled = [tree_sum([at(i, j) * marked[j] for j in range(8)]) for i in range(8)]
+    swept = [None] * k
+    fresh = -scaled[7]
+    for i in range(7):
+        fresh = jnp.where(sub == i, -scaled[i], fresh)
+    swept.append(fresh)
+    for v in range(k + 1, len(groups)):
+        spread = columns.get(v) or spread_columns(groups[v], start)
+        swept.append(
+            jnp.where(inside, 0.0, groups[v]) + tree_sum([spread[i] * scaled[i] for i in range(8)])
+        )
+    return swept, next_columns
+
+
+def solve(matrix, lower, scaled_lower, shelf, rhs):
     half = matrix.shape[0] // 2
     dot = functools.partial(jnp.dot, precision=highest, preferred_element_type=f32)
     count = half // 8
+    lane = iota((8, half), 1)
     groups = [matrix[8 * v : 8 * v + 8, 0:half] for v in range(count)]
     groups.append(jnp.broadcast_to(rhs[:, 0:half], (8, half)))
+    columns = spread_columns(groups[0], 0)
     for k in range(count):
-        groups = sweep(groups, k)
-    for v in range(count):
-        inverse[8 * v : 8 * v + 8, :] = groups[v]
+        pivots = groups[k]
+        groups, columns = sweep(groups, k, columns, shelf)
+        done, own = lane < 8 * k + 8, lane >= 8 * k
+        unit = jnp.where(lane == 8 * k + iota((8, half), 0), -1.0, 0.0)
+        lower[8 * k : 8 * k + 8, :] = jnp.where(done, jnp.where(own, unit, pivots), 0.0)
+        scaled_lower[8 * k : 8 * k + 8, :] = jnp.where(done, groups[k], 0.0)
     top = groups[count]
-    cross = -dot(matrix[half : 2 * half, 0:half], inverse[...])
+    cross = dot(
+        lax.dot_general(
+            matrix[half : 2 * half, 0:half], lower[...], (((1,), (1,)), ((), ())),
+            precision=highest, preferred_element_type=f32,
+        ),
+        scaled_lower[...],
+    )
     rest = matrix[half : 2 * half, half : 2 * half] - dot(cross, matrix[0:half, half : 2 * half])
     groups = [rest[8 * v : 8 * v + 8, :] for v in range(count)]
     groups.append(rhs[:, half : 2 * half] - dot(top, matrix[0:half, half : 2 * half]))
+    columns = spread_columns(groups[0], 0)
     for k in range(count):
-        groups = sweep(groups, k)
+        groups, columns = sweep(groups, k, columns, shelf)
     bottom = groups[count]
     top = top - dot(bottom, cross)
     return jnp.concatenate([top[0:1, :], bottom[0:1, :]], axis=1)
 
 
-def solve_kernel(rows_ref, gram_ref, energy_ref, weights_ref, update_ref, work, inverse):
+def solve_kernel(rows_ref, gram_ref, energy_ref, weights_ref, update_ref, work, lower, scaled_lower, shelf):
     mats, share, peers, samples, width = rows_ref.shape
     total = peers * samples
     me = lax.axis_index("samp")
@@ -371,7 +399,7 @@
     held = iota((peers, total), 1) // samples == iota((peers, total), 0)
     energy = jnp.sum(jnp.where(held, every, 0.0), axis=0, keepdims=True)
     eps = (energy - jnp.mean(energy)) / jnp.sqrt(f32(total))
-    weights = solve(work, inverse, eps)
+    weights = solve(work, lower, scaled_lower, shelf, eps)
     weights_ref[...] = pltpu.roll(weights, total - me * samples, 1)[:, 0:samples]
     coeffs = weights - jnp.mean(weights)
     first = coeffs.astype(jnp.bfloat16)
@@ -400,7 +428,12 @@
         ),
         in_specs=[vmem, vmem, vmem],
         out_specs=(vmem, vmem),
-        scratch_shapes=[pltpu.VMEM((total, total), f32), pltpu.VMEM((total // 2, total // 2), f32)],
+        scratch_shapes=[
+            pltpu.VMEM((total, total), f32),
+            pltpu.VMEM((total // 2, total // 2), f32),
+            pltpu.VMEM((total // 2, total // 2), f32),
+            pltpu.VMEM((2, 136, total // 2), f32),
+        ],
         compiler_params=pltpu.CompilerParams(vmem_limit_bytes=20 << 20),
     )(rows, gram, energy)
 

time: 63.5 us -> 59.9 us (0.943)
  Pallas kernels: 62.8 us -> 59.1 us
    pallas_call x1, Pallas kernels: 12.4 us -> 8.75 us  [solve_and_update(): pl.pallas_call(solve_kernel, out_shape=(jax.ShapeDtypeStruct((1, samples)...]
where the time goes in v5:
time: 59.9 us; the launch traced here: 59.7 us
  Pallas kernels  59.1 us (99%)
  between operations  0.64 us (1%)
    pallas_call x1, Pallas kernels, gram_and_rows(): pl.pallas_call(functools.partial(gram_kernel, peers, layers), out_shape=(...  50.3 us
    pallas_call x1, Pallas kernels, solve_and_update(): pl.pallas_call(solve_kernel, out_shape=(jax.ShapeDtypeStruct((1, samples)...  8.75 us

profile of v5, /device:TPU:1, one launch (start us, length us, event | category | flops | bytes accessed | tf_op | source)
XLA Modules:
  0.0 59.7 jit_solution(13238346616623842108)
XLA Ops:
  0.6 50.3 %shard_map.59 = (bf16[2,8,32,8,256]{4,3,2,1,0:T(8,128)(2,1)S(1)}, f32[256,256]{1,0:T(8,128)S(1)}, f32[32,1,256]{2,1,0:T(1,128)S(1)}) custom-call(s32[8,256]{1,0:T(8,128)} %spins_hbm.1, f32[1,8]{1,0:T(1,128)} %bitcast.2, bf16[8,2,256,256]{3,2,1,0:T(8,128)(2,1)} %act_hbm.1, bf16[8,2,256,256]{3,2,1,0:T(8,128)(2,1)} %cot_hbm.1), custom_call_target="tpu_custom_call" | custom-call | tf_op jit(solution)/shard_map/pallas_call | solution.py:227
  51.0 8.7 %shard_map.60 = (f32[1,8]{1,0:T(1,128)}, f32[2,8,256]{2,1,0:T(8,128)}) custom-call(bf16[2,8,32,8,256]{4,3,2,1,0:T(8,128)(2,1)S(1)} %get-tuple-element.7.rows_ref, f32[256,256]{1,0:T(8,128)S(1)} %get-tuple-element.8.gram_ref, f32[32,1,256]{2,1,0:T(1,128)S(1)} %get-tuple-element.9.energy_ref), custom_call_target="tpu_custom_call" | custom-call | tf_op jit(solution)/shard_map/pallas_call | solution.py:423

commit v6 on v5

--- a/solution.py
+++ b/solution.py
@@ -14,6 +14,11 @@
 f32 = jnp.float32
 CHIPS = (2, 2), (2, 1), (1, 2), (2, 3), (3, 2), (1, 1), (3, 3), (1, 3), (3, 1), (2, 0), (0, 2), (1, 0), (3, 0), (0, 1), (0, 3)
 FAR_FIRST = [(y, z, c) for c in (0, 1) for y, z in CHIPS] + [(0, 0, 1)]
+
+CHIP_STEPS = sorted(
+    [(y, z, x) for y in range(4) for z in range(4) for x in range(4) if y or z or x],
+    key=lambda step: -sum(min(hop, 4 - hop) for hop in step),
+)
 
 
 def peer_at(me, step):
@@ -50,7 +55,7 @@
     rows_ref, gram_ref, energy_ref,
     spins, offdiag, act, cot, wide, outgoing, own_gram, pieces, sums, spread, energy,
     small_sem, energy_send, energy_recv,
-    in_sem, own_sem, row_send, row_recv, piece_send, piece_recv,
+    planes, in_sem, own_sem, row_send, row_recv, piece_send, piece_recv,
     sum_send, sum_recv, spread_send, spread_recv,
 ):
     samples, mats, sites, width = act.shape
@@ -58,40 +63,33 @@
     me = lax.axis_index("samp")
     layer = lax.axis_index("layer")
 
-    def loads(s):
+    def loads(m, s):
         return (
-            pltpu.make_async_copy(act_hbm.at[s], act.at[s], in_sem.at[0, s]),
-            pltpu.make_async_copy(cot_hbm.at[s], cot.at[s], in_sem.at[1, s]),
+            pltpu.make_async_copy(act_hbm.at[s, m], act.at[s, m], in_sem.at[0, m, s]),
+            pltpu.make_async_copy(cot_hbm.at[s, m], cot.at[s, m], in_sem.at[1, m, s]),
         )
 
     small = (
         pltpu.make_async_copy(spins_hbm, spins, small_sem.at[0]),
         pltpu.make_async_copy(offdiag_hbm, offdiag, small_sem.at[1]),
     )
-    for load in small:
-        load.start()
-    for s in range(samples):
-        for load in loads(s):
-            load.start()
-
+    steps = [peer_at(me, step) for step in FAR_FIRST]
     barrier = pltpu.get_barrier_semaphore()
-
-    def greet(i, carry):
-        pl.semaphore_signal(
-            barrier, inc=1, device_id={"samp": lax.rem(me + i, peers)}, device_id_type=MESH
-        )
-        return carry
-
-    lax.fori_loop(1, peers, greet, 0)
-    for i in range(1, layers):
-        pl.semaphore_signal(
-            barrier, inc=1, device_id={"layer": lax.rem(layer + i, layers)}, device_id_type=MESH
-        )
-
+    for peer in steps:
+        pl.semaphore_signal(barrier, inc=1, device_id={"samp": peer}, device_id_type=MESH)
+    others = [lax.rem(layer + i, layers) for i in (2, 1, 3)]
+    for other in others:
+        pl.semaphore_signal(barrier, inc=1, device_id={"layer": other}, device_id_type=MESH)
+    for m in range(mats):
+        for s in range(samples):
+            for load in loads(m, s):
+                load.start()
+        if m == 0:
+            for load in small:
+                load.start()
     for load in small:
         load.wait()
     energy[...] = local_energy(spins[...], offdiag[...])
-    steps = [peer_at(me, step) for step in FAR_FIRST]
 
     def energy_copy(peer):
         return pltpu.make_async_remote_copy(
@@ -115,9 +113,8 @@
 
     for m in range(mats):
         for s in range(samples):
-            if m == 0:
-                for load in loads(s):
-                    load.wait()
+            for load in loads(m, s):
+                load.wait()
             jac = lax.dot_general(
                 act[s, m], cot[s, m], (((0,), (0,)), ((), ())), preferred_element_type=f32
             )
@@ -130,6 +127,8 @@
                 outgoing[m, k, :, :, h * 128 : (h + 1) * 128] = block.reshape(share, samples, 128).astype(jnp.bfloat16)
         if m == 0:
             pl.semaphore_wait(barrier, peers + layers - 2)
+            for other in others:
+                pl.semaphore_signal(planes, inc=1, device_id={"layer": other}, device_id_type=MESH)
         for peer in steps:
             row_copy(m, peer).start()
         if m == 0:
@@ -149,70 +148,73 @@
                 rows, rows, (((1,), (1,)), ((), ())), preferred_element_type=f32
             )
             total = term if total is None else total + term
-        if m == 0:
-            own_gram[...] = total
-        else:
-            own_gram[...] = own_gram[...] + total
-
-    def piece_copy(peer):
+        for h in range(2):
+            part = total[:, h * 128 : (h + 1) * 128]
+            own_gram[h] = part if m == 0 else own_gram[h] + part
+    pl.semaphore_wait(planes, layers - 1)
+
+    core = me % 2
+    chip = me // 2 * layers + layer
+
+    def tile_of(q):
+        return q % 2, pl.ds(pl.multiple_of(q // 2 * 8, 8), 8)
+
+    def chip_at(step):
+        y, z, x = step
+        place = (me // 8 + y) % 4 * 4 + (me // 2 % 4 + z) % 4
+        return place * 2 + core, (layer + x) % layers, place * layers + (layer + x) % layers
+
+    chips = [chip_at(step) for step in CHIP_STEPS]
+
+    def piece_copy(samp, plane, q):
         return pltpu.make_async_remote_copy(
-            src_ref=own_gram.at[pl.ds(pl.multiple_of(peer * samples, samples), samples)],
-            dst_ref=pieces.at[me],
+            src_ref=own_gram.at[tile_of(q)],
+            dst_ref=pieces.at[chip],
             send_sem=piece_send,
             recv_sem=piece_recv,
-            device_id={"samp": peer},
+            device_id={"samp": samp, "layer": plane},
             device_id_type=MESH,
         )
 
-    for peer in steps:
-        piece_copy(peer).start()
-    pieces[me] = own_gram[pl.ds(pl.multiple_of(me * samples, samples), samples)]
-    many = pieces.at[0 : peers - 1]
+    for samp, plane, q in chips:
+        piece_copy(samp, plane, q).start()
+    pieces[chip] = own_gram[tile_of(chip)]
+    many = pieces.at[0 : len(chips)]
     pltpu.make_async_copy(many, many, piece_recv).wait()
-    sums[layer] = jnp.sum(pieces[...], axis=0)
-
-    def sum_copy(i):
-        return pltpu.make_async_remote_copy(
-            src_ref=sums.at[layer],
-            dst_ref=sums.at[layer],
-            send_sem=sum_send.at[i],
-            recv_sem=sum_recv.at[i],
-            device_id={"layer": lax.rem(layer + i, layers)},
-            device_id_type=MESH,
-        )
-
-    for i in (2, 1, 3):
-        sum_copy(i).start()
-    for i in range(1, layers):
-        sum_copy(i).wait_recv()
-    spread[...] = jnp.sum(sums[...], axis=0)
-
-    mine = pl.ds(pl.multiple_of(me * samples, samples), samples)
-
-    def spread_copy(peer):
+    sums[core] = jnp.sum(pieces[...], axis=0)
+    sibling = pltpu.make_async_remote_copy(
+        src_ref=sums.at[core],
+        dst_ref=sums.at[core],
+        send_sem=sum_send,
+        recv_sem=sum_recv,
+        device_id={"samp": me + 1 - 2 * core},
+        device_id_type=MESH,
+    )
+    sibling.start()
+    sibling.wait()
+    spread[...] = sums[0] + sums[1]
+
+    def spread_copy(samp, plane):
         return pltpu.make_async_remote_copy(
             src_ref=spread,
-            dst_ref=gram_ref.at[mine],
+            dst_ref=gram_ref.at[tile_of(chip)],
             send_sem=spread_send,
             recv_sem=spread_recv,
-            device_id={"samp": peer},
+            device_id={"samp": samp, "layer": plane},
             device_id_type=MESH,
         )
 
-    for peer in steps:
-        spread_copy(peer).start()
-    gram_ref[mine] = spread[...]
+    for samp, plane, q in chips:
+        spread_copy(samp, plane).start()
+    gram_ref[tile_of(chip)] = spread[...]
     for m in range(mats):
         many = outgoing.at[m, 0 : peers - 1]
         pltpu.make_async_copy(many, many, row_send.at[m]).wait()
     many = energy_ref.at[0 : peers - 1]
     pltpu.make_async_copy(many, many, energy_send).wait()
     pltpu.make_async_copy(many, many, energy_recv).wait()
-    many = own_gram.at[0 : (peers - 1) * samples]
+    many = pieces.at[0 : len(chips)]
     pltpu.make_async_copy(many, many, piece_send).wait()
-    for i in range(1, layers):
-        sum_copy(i).wait_send()
-    many = gram_ref.at[0 : (peers - 1) * samples]
     pltpu.make_async_copy(many, many, spread_recv).wait()
     pltpu.make_async_copy(many, many, spread_send).wait()
 
@@ -228,7 +230,7 @@
         functools.partial(gram_kernel, peers, layers),
         out_shape=(
             jax.ShapeDtypeStruct((mats, share, peers, samples, width), bf16),
-            jax.ShapeDtypeStruct((total, total), f32),
+            jax.ShapeDtypeStruct((2, total, 128), f32),
             jax.ShapeDtypeStruct((peers, 1, total), f32),
         ),
         in_specs=[pl.BlockSpec(memory_space=pltpu.HBM)] * 4,
@@ -240,22 +242,23 @@
             pltpu.VMEM(cotangents.shape, bf16),
             pltpu.VMEM((width // 128 * width * samples, 128), f32),
             pltpu.VMEM((mats, peers, share, samples, width), bf16),
-            pltpu.VMEM((total, total), f32),
-            pltpu.VMEM((peers, samples, total), f32),
-            pltpu.VMEM((layers, samples, total), f32),
-            pltpu.VMEM((samples, total), f32),
+            pltpu.VMEM((2, total, 128), f32),
+            pltpu.VMEM((peers // 2 * layers, 8, 128), f32),
+            pltpu.VMEM((2, 8, 128), f32),
+            pltpu.VMEM((8, 128), f32),
             pltpu.VMEM((1, total), f32),
             dma((2,)),
             dma,
             dma,
-            dma((2, samples)),
+            pltpu.SemaphoreType.REGULAR,
+            dma((2, mats, samples)),
             dma((mats,)),
             dma((mats,)),
             dma((mats,)),
             dma,
             dma,
-            dma((layers,)),
-            dma((layers,)),
+            dma,
+            dma,
             dma,
             dma,
         ],
@@ -384,7 +387,7 @@
     mats, share, peers, samples, width = rows_ref.shape
     total = peers * samples
     me = lax.axis_index("samp")
-    raw = gram_ref[...]
+    raw = jnp.concatenate([gram_ref[0], gram_ref[1]], axis=1)
     means = jnp.mean(raw, axis=1, keepdims=True)
     diagonal = iota((total, total), 0) == iota((total, total), 1)
 

time: 59.9 us -> 59.7 us (level)
  no operation moved by 1% of the time
where the time goes in v6:
time: 59.7 us; the launch traced here: 59.5 us
  Pallas kernels  58.9 us (99%)
  between operations  0.64 us (1%)
    pallas_call x1, Pallas kernels, gram_and_rows(): pl.pallas_call(functools.partial(gram_kernel, peers, layers), out_shape=(...  50.2 us
    pallas_call x1, Pallas kernels, solve_and_update(): pl.pallas_call(solve_kernel, out_shape=(jax.ShapeDtypeStruct((1, samples)...  8.75 us

profile of v6, /device:TPU:1, one launch (start us, length us, event | category | flops | bytes accessed | tf_op | source)
XLA Modules:
  0.0 59.5 jit_solution(12418873490592930906)
XLA Ops:
  0.6 50.2 %shard_map.59 = (bf16[2,8,32,8,256]{4,3,2,1,0:T(8,128)(2,1)S(1)}, f32[2,256,128]{2,1,0:T(8,128)S(1)}, f32[32,1,256]{2,1,0:T(1,128)S(1)}) custom-call(s32[8,256]{1,0:T(8,128)} %spins_hbm.1, f32[1,8]{1,0:T(1,128)} %bitcast.2, bf16[8,2,256,256]{3,2,1,0:T(8,128)(2,1)} %act_hbm.1, bf16[8,2,256,256]{3,2,1,0:T(8,128)(2,1)} %cot_hbm.1), custom_call_target="tpu_custom_call" | custom-call | tf_op jit(solution)/shard_map/pallas_call | solution.py:229
  50.8 8.7 %shard_map.60 = (f32[1,8]{1,0:T(1,128)}, f32[2,8,256]{2,1,0:T(8,128)}) custom-call(bf16[2,8,32,8,256]{4,3,2,1,0:T(8,128)(2,1)S(1)} %get-tuple-element.7.rows_ref, f32[2,256,128]{2,1,0:T(8,128)S(1)} %get-tuple-element.8.gram_ref, f32[32,1,256]{2,1,0:T(1,128)S(1)} %get-tuple-element.9.energy_ref), custom_call_target="tpu_custom_call" | custom-call | tf_op jit(solution)/shard_map/pallas_call | solution.py:426

commit v7 on v6

--- a/solution.py
+++ b/solution.py
@@ -15,9 +15,16 @@
 CHIPS = (2, 2), (2, 1), (1, 2), (2, 3), (3, 2), (1, 1), (3, 3), (1, 3), (3, 1), (2, 0), (0, 2), (1, 0), (3, 0), (0, 1), (0, 3)
 FAR_FIRST = [(y, z, c) for c in (0, 1) for y, z in CHIPS] + [(0, 0, 1)]
 
-CHIP_STEPS = sorted(
-    [(y, z, x) for y in range(4) for z in range(4) for x in range(4) if y or z or x],
-    key=lambda step: -sum(min(hop, 4 - hop) for hop in step),
+OWNING = 3
+
+
+def far_first(steps):
+    return sorted(steps, key=lambda step: -sum(min(hop, 4 - hop) for hop in step))
+
+
+PLACE_STEPS = far_first([(y, z) for y in range(4) for z in range(4) if y or z])
+CHIP_STEPS = far_first(
+    [(y, z, x) for y in range(4) for z in range(4) for x in range(4) if y or z or x]
 )
 
 
@@ -47,6 +54,10 @@
     energy = bonds + jnp.sum(jnp.where(diagonal, square, 0.0), axis=1, keepdims=True)
     repeated = iota((samples, sites), 1) % samples == iota((samples, sites), 0)
     return jnp.sum(jnp.where(repeated, energy, 0.0), axis=0, keepdims=True)
+
+
+def products(a, b):
+    return lax.dot_general(a, b, (((1,), (1,)), ((), ())), preferred_element_type=f32)
 
 
 def gram_kernel(
@@ -141,82 +152,97 @@
         pltpu.make_async_copy(outgoing.at[m, me], rows_ref.at[m, :, me], own_sem.at[m]).wait()
         many = rows_ref.at[m, :, 0 : peers - 1]
         pltpu.make_async_copy(many, many, row_recv.at[m]).wait()
-        total = None
+        left, right = None, None
         for r in range(share):
             rows = rows_ref[m, r].reshape(peers * samples, width)
-            term = lax.dot_general(
-                rows, rows, (((1,), (1,)), ((), ())), preferred_element_type=f32
-            )
-            total = term if total is None else total + term
-        for h in range(2):
-            part = total[:, h * 128 : (h + 1) * 128]
-            own_gram[h] = part if m == 0 else own_gram[h] + part
+            halves = rows[: peers * samples // 2], rows[peers * samples // 2 :]
+            first = products(rows, halves[0])
+            second = products(halves[1], halves[1])
+            left, right = (first, second) if r == 0 else (left + first, right + second)
+        parts = jnp.concatenate([left, right], axis=0)
+        own_gram[...] = parts if m == 0 else own_gram[...] + parts
     pl.semaphore_wait(planes, layers - 1)
 
     core = me % 2
     chip = me // 2 * layers + layer
 
-    def tile_of(q):
-        return q % 2, pl.ds(pl.multiple_of(q // 2 * 8, 8), 8)
-
-    def chip_at(step):
-        y, z, x = step
-        place = (me // 8 + y) % 4 * 4 + (me // 2 % 4 + z) % 4
-        return place * 2 + core, (layer + x) % layers, place * layers + (layer + x) % layers
-
-    chips = [chip_at(step) for step in CHIP_STEPS]
-
-    def piece_copy(samp, plane, q):
+    place = me // 2
+
+    def tile_at(owner_place, plane):
+        return pl.ds(pl.multiple_of((owner_place * OWNING + plane) * 8, 8), 8)
+
+    def moved(y, z):
+        return (place // 4 + y) % 4 * 4 + (place % 4 + z) % 4
+
+    def piece_copy(there, plane):
         return pltpu.make_async_remote_copy(
-            src_ref=own_gram.at[tile_of(q)],
+            src_ref=own_gram.at[tile_at(there, plane)],
             dst_ref=pieces.at[chip],
             send_sem=piece_send,
             recv_sem=piece_recv,
-            device_id={"samp": samp, "layer": plane},
+            device_id={"samp": there * 2 + core, "layer": plane},
             device_id_type=MESH,
         )
 
-    for samp, plane, q in chips:
-        piece_copy(samp, plane, q).start()
-    pieces[chip] = own_gram[tile_of(chip)]
-    many = pieces.at[0 : len(chips)]
-    pltpu.make_async_copy(many, many, piece_recv).wait()
-    sums[core] = jnp.sum(pieces[...], axis=0)
-    sibling = pltpu.make_async_remote_copy(
-        src_ref=sums.at[core],
-        dst_ref=sums.at[core],
-        send_sem=sum_send,
-        recv_sem=sum_recv,
-        device_id={"samp": me + 1 - 2 * core},
-        device_id_type=MESH,
-    )
-    sibling.start()
-    sibling.wait()
-    spread[...] = sums[0] + sums[1]
-
-    def spread_copy(samp, plane):
-        return pltpu.make_async_remote_copy(
-            src_ref=spread,
-            dst_ref=gram_ref.at[tile_of(chip)],
-            send_sem=spread_send,
-            recv_sem=spread_recv,
-            device_id={"samp": samp, "layer": plane},
+    for y, z in PLACE_STEPS:
+        for plane in range(OWNING):
+            piece_copy(moved(y, z), plane).start()
+    for other in others:
+
+        @pl.when(other < OWNING)
+        def _(other=other):
+            piece_copy(place, other).start()
+
+    def await_tiles(sem, ref, count):
+        many = ref.at[0 : count * 8]
+        pltpu.make_async_copy(many, many, sem).wait()
+
+    owns = layer < OWNING
+    tiles = (peers // 2) * OWNING
+
+    @pl.when(owns)
+    def _():
+        pieces[chip] = own_gram[tile_at(place, layer)]
+        many = pieces.at[0 : len(CHIP_STEPS)]
+        pltpu.make_async_copy(many, many, piece_recv).wait()
+        sums[core] = jnp.sum(pieces[...], axis=0)
+        sibling = pltpu.make_async_remote_copy(
+            src_ref=sums.at[core],
+            dst_ref=sums.at[core],
+            send_sem=sum_send,
+            recv_sem=sum_recv,
+            device_id={"samp": me + 1 - 2 * core},
             device_id_type=MESH,
         )
-
-    for samp, plane, q in chips:
-        spread_copy(samp, plane).start()
-    gram_ref[tile_of(chip)] = spread[...]
+        sibling.start()
+        sibling.wait()
+        spread[...] = sums[0] + sums[1]
+        for y, z, x in CHIP_STEPS:
+            pltpu.make_async_remote_copy(
+                src_ref=spread,
+                dst_ref=gram_ref.at[tile_at(place, layer)],
+                send_sem=spread_send,
+                recv_sem=spread_recv,
+                device_id={"samp": moved(y, z) * 2 + core, "layer": (layer + x) % layers},
+                device_id_type=MESH,
+            ).start()
+        gram_ref[tile_at(place, layer)] = spread[...]
+        await_tiles(piece_send, own_gram, tiles - 1)
+        await_tiles(spread_recv, gram_ref, tiles - 1)
+        many = pieces.at[0 : len(CHIP_STEPS)]
+        pltpu.make_async_copy(many, many, spread_send).wait()
+
+    @pl.when(jnp.logical_not(owns))
+    def _():
+        await_tiles(piece_send, own_gram, tiles)
+        await_tiles(spread_recv, gram_ref, tiles)
+
     for m in range(mats):
         many = outgoing.at[m, 0 : peers - 1]
         pltpu.make_async_copy(many, many, row_send.at[m]).wait()
     many = energy_ref.at[0 : peers - 1]
     pltpu.make_async_copy(many, many, energy_send).wait()
     pltpu.make_async_copy(many, many, energy_recv).wait()
-    many = pieces.at[0 : len(chips)]
-    pltpu.make_async_copy(many, many, piece_send).wait()
-    pltpu.make_async_copy(many, many, spread_recv).wait()
-    pltpu.make_async_copy(many, many, spread_send).wait()
 
 
 def gram_and_rows(spins, activations, cotangents, offdiag):
@@ -230,7 +256,7 @@
         functools.partial(gram_kernel, peers, layers),
         out_shape=(
             jax.ShapeDtypeStruct((mats, share, peers, samples, width), bf16),
-            jax.ShapeDtypeStruct((2, total, 128), f32),
+            jax.ShapeDtypeStruct((total // 2 * 3, 128), f32),
             jax.ShapeDtypeStruct((peers, 1, total), f32),
         ),
         in_specs=[pl.BlockSpec(memory_space=pltpu.HBM)] * 4,
@@ -242,7 +268,7 @@
             pltpu.VMEM(cotangents.shape, bf16),
             pltpu.VMEM((width // 128 * width * samples, 128), f32),
             pltpu.VMEM((mats, peers, share, samples, width), bf16),
-            pltpu.VMEM((2, total, 128), f32),
+            pltpu.VMEM((total // 2 * 3, 128), f32),
             pltpu.VMEM((peers // 2 * layers, 8, 128), f32),
             pltpu.VMEM((2, 8, 128), f32),
             pltpu.VMEM((8, 128), f32),
@@ -268,31 +294,50 @@
     )(*(pltpu.with_memory_space_constraint(a, pltpu.HBM) for a in (spins, offdiag[None, :], activations, cotangents)))
 
 
-def minus_inverse(entry, order):
-    at = lambda i, j: entry[min(i, j), max(i, j)]
-    for p in range(0, order, 2):
+def eliminate(entry):
+    entry = dict(entry)
+    inverses, gain = [], {}
+    for p in range(0, 8, 2):
         q = p + 1
         first, cross, second = entry[p, p], entry[p, q], entry[q, q]
         scale = 1.0 / (first * second - cross * cross)
-        inv_pp, inv_pq, inv_qq = second * scale, cross * scale, first * scale
-        others = [i for i in range(order) if i not in (p, q)]
-        gain = {
-            i: (
-                at(i, p) * inv_pp - at(i, q) * inv_pq,
-                at(i, q) * inv_qq - at(i, p) * inv_pq,
-            )
-            for i in others
-        }
-        fresh = {}
-        for x, i in enumerate(others):
-            for j in others[x:]:
-                fresh[i, j] = entry[i, j] - (gain[i][0] * at(j, p) + gain[i][1] * at(j, q))
-            fresh[min(i, p), max(i, p)] = gain[i][0]
-            fresh[min(i, q), max(i, q)] = gain[i][1]
-        fresh[p, p], fresh[p, q], fresh[q, q] = -inv_pp, inv_pq, -inv_qq
-        entry = fresh
-        at = lambda i, j, entry=entry: entry[min(i, j), max(i, j)]
-    return entry
+        inv = second * scale, cross * scale, first * scale
+        inverses.append(inv)
+        later = range(p + 2, 8)
+        for i in later:
+            at_p, at_q = entry[p, i], entry[q, i]
+            gain[i, p] = at_p * inv[0] - at_q * inv[1], at_q * inv[2] - at_p * inv[1]
+        for i in later:
+            for j in range(i, 8):
+                entry[i, j] = entry[i, j] - (gain[i, p][0] * entry[p, j] + gain[i, p][1] * entry[q, j])
+    return inverses, gain
+
+
+def forward(gain, values):
+    values = list(values)
+    for p in range(0, 8, 2):
+        for i in range(p + 2, 8):
+            by_p, by_q = gain[i, p]
+            values[i] = values[i] - (by_p * values[p] + by_q * values[p + 1])
+    return values
+
+
+def scale_pairs(inverses, values):
+    scaled = []
+    for p in range(0, 8, 2):
+        pp, pq, qq = inverses[p // 2]
+        first, second = values[p], values[p + 1]
+        scaled += [first * pp - second * pq, second * qq - first * pq]
+    return scaled
+
+
+def backward(gain, values):
+    values = list(values)
+    for p in range(6, -1, -2):
+        for i in range(7, p + 1, -1):
+            values[p] = values[p] - gain[i, p][0] * values[i]
+            values[p + 1] = values[p + 1] - gain[i, p][1] * values[i]
+    return values
 
 
 def tree_sum(terms):
@@ -319,32 +364,32 @@
 
     put(0, own_columns)
     entry = {(i, j): spread_row(0, j, i) for i in range(8) for j in range(i, 8)}
-    entry = minus_inverse(entry, 8)
-    at = lambda i, j: entry[min(i, j), max(i, j)]
+    inverses, gain = eliminate(entry)
     next_columns, columns = None, {}
     if start + 8 < shape[1]:
         near = columns[k + 1] = spread_columns(groups[k + 1], start)
-        put(64, near)
-        gains = [tree_sum([at(i, a) * near[a] for a in range(8)]) for i in range(8)]
+        reduced = forward(gain, near)
+        put(64, reduced)
+        gains = scale_pairs(inverses, reduced)
         old = spread_columns(groups[k + 1], start + 8)
         next_columns = [
-            old[j] + tree_sum([gains[i] * spread_row(64, i, j) for i in range(8)]) for j in range(8)
+            old[j] - tree_sum([gains[i] * spread_row(64, i, j) for i in range(8)]) for j in range(8)
         ]
     put(128, [groups[k]])
     inside = (lane >= start) & (lane < start + 8)
     marked = [
         jnp.where(inside, jnp.where(lane == start + j, -1.0, 0.0), spread_row(128, 0, j)) for j in range(8)
     ]
-    scaled = [tree_sum([at(i, j) * marked[j] for j in range(8)]) for i in range(8)]
+    scaled = backward(gain, scale_pairs(inverses, forward(gain, marked)))
     swept = [None] * k
-    fresh = -scaled[7]
+    fresh = scaled[7]
     for i in range(7):
-        fresh = jnp.where(sub == i, -scaled[i], fresh)
+        fresh = jnp.where(sub == i, scaled[i], fresh)
     swept.append(fresh)
     for v in range(k + 1, len(groups)):
         spread = columns.get(v) or spread_columns(groups[v], start)
         swept.append(
-            jnp.where(inside, 0.0, groups[v]) + tree_sum([spread[i] * scaled[i] for i in range(8)])
+            jnp.where(inside, 0.0, groups[v]) - tree_sum([spread[i] * scaled[i] for i in range(8)])
         )
     return swept, next_columns
 
@@ -387,7 +432,15 @@
     mats, share, peers, samples, width = rows_ref.shape
     total = peers * samples
     me = lax.axis_index("samp")
-    raw = jnp.concatenate([gram_ref[0], gram_ref[1]], axis=1)
+    half = total // 2
+    corner = gram_ref[half:total, :]
+    raw = jnp.concatenate(
+        [
+            jnp.concatenate([gram_ref[0:half, :], corner.T], axis=1),
+            jnp.concatenate([corner, gram_ref[total:, :]], axis=1),
+        ],
+        axis=0,
+    )
     means = jnp.mean(raw, axis=1, keepdims=True)
     diagonal = iota((total, total), 0) == iota((total, total), 1)
 

time: 59.7 us -> 58.2 us (0.975)
  Pallas kernels: 58.9 us -> 57.5 us
    pallas_call x1, Pallas kernels: 8.75 us -> 7.73 us  [solve_and_update(): pl.pallas_call(solve_kernel, out_shape=(jax.ShapeDtypeStruct((1, samples)...]
where the time goes in v7:
time: 58.2 us; the launch traced here: 58.1 us
  Pallas kernels  57.5 us (99%)
  between operations  0.64 us (1%)
    pallas_call x1, Pallas kernels, gram_and_rows(): pl.pallas_call(functools.partial(gram_kernel, peers, layers), out_shape=(...  49.7 us
    pallas_call x1, Pallas kernels, solve_and_update(): pl.pallas_call(solve_kernel, out_shape=(jax.ShapeDtypeStruct((1, samples)...  7.73 us

profile of v7, /device:TPU:1, one launch (start us, length us, event | category | flops | bytes accessed | tf_op | source)
XLA Modules:
  0.0 58.1 jit_solution(11535809451615402723)
XLA Ops:
  0.6 49.7 %shard_map.59 = (bf16[2,8,32,8,256]{4,3,2,1,0:T(8,128)(2,1)S(1)}, f32[384,128]{1,0:T(8,128)S(1)}, f32[32,1,256]{2,1,0:T(1,128)S(1)}) custom-call(s32[8,256]{1,0:T(8,128)} %spins_hbm.1, f32[1,8]{1,0:T(1,128)} %bitcast.2, bf16[8,2,256,256]{3,2,1,0:T(8,128)(2,1)} %act_hbm.1, bf16[8,2,256,256]{3,2,1,0:T(8,128)(2,1)} %cot_hbm.1), custom_call_target="tpu_custom_call" | custom-call | tf_op jit(solution)/shard_map/pallas_call | solution.py:255
  50.4 7.7 %shard_map.60 = (f32[1,8]{1,0:T(1,128)}, f32[2,8,256]{2,1,0:T(8,128)}) custom-call(bf16[2,8,32,8,256]{4,3,2,1,0:T(8,128)(2,1)S(1)} %get-tuple-element.7.rows_ref, f32[384,128]{1,0:T(8,128)S(1)} %get-tuple-element.8.gram_ref, f32[32,1,256]{2,1,0:T(1,128)S(1)} %get-tuple-element.9.energy_ref), custom_call_target="tpu_custom_call" | custom-call | tf_op jit(solution)/shard_map/pallas_call | solution.py:479

commit v8 on v7

--- a/solution.py
+++ b/solution.py
@@ -56,6 +56,13 @@
     return jnp.sum(jnp.where(repeated, energy, 0.0), axis=0, keepdims=True)
 
 
+def whole_rows(rows_ref, m, r):
+    _, halves, peers, _, samples, lanes = rows_ref.shape
+    return jnp.concatenate(
+        [rows_ref[m, h, :, r].reshape(peers * samples, lanes) for h in range(halves)], axis=1
+    )
+
+
 def products(a, b):
     return lax.dot_general(a, b, (((1,), (1,)), ((), ())), preferred_element_type=f32)
 
@@ -64,13 +71,15 @@
     peers, layers,
     spins_hbm, offdiag_hbm, act_hbm, cot_hbm,
     rows_ref, gram_ref, energy_ref,
-    spins, offdiag, act, cot, wide, outgoing, own_gram, pieces, sums, spread, energy,
+    spins, offdiag, act, cot, wide, outgoing, own_gram, pieces, spread, energy,
     small_sem, energy_send, energy_recv,
     planes, in_sem, own_sem, row_send, row_recv, piece_send, piece_recv,
-    sum_send, sum_recv, spread_send, spread_recv,
+    spread_send, spread_recv,
 ):
     samples, mats, sites, width = act.shape
     share = width // peers
+    halves_of_rows = width // 128
+    parts_of_rows = [(m, h) for m in range(mats) for h in range(halves_of_rows)]
     me = lax.axis_index("samp")
     layer = lax.axis_index("layer")
 
@@ -85,12 +94,6 @@
         pltpu.make_async_copy(offdiag_hbm, offdiag, small_sem.at[1]),
     )
     steps = [peer_at(me, step) for step in FAR_FIRST]
-    barrier = pltpu.get_barrier_semaphore()
-    for peer in steps:
-        pl.semaphore_signal(barrier, inc=1, device_id={"samp": peer}, device_id_type=MESH)
-    others = [lax.rem(layer + i, layers) for i in (2, 1, 3)]
-    for other in others:
-        pl.semaphore_signal(barrier, inc=1, device_id={"layer": other}, device_id_type=MESH)
     for m in range(mats):
         for s in range(samples):
             for load in loads(m, s):
@@ -98,6 +101,12 @@
         if m == 0:
             for load in small:
                 load.start()
+    barrier = pltpu.get_barrier_semaphore()
+    for peer in steps:
+        pl.semaphore_signal(barrier, inc=1, device_id={"samp": peer}, device_id_type=MESH)
+    others = [lax.rem(layer + i, layers) for i in (2, 1, 3)]
+    for other in others:
+        pl.semaphore_signal(barrier, inc=1, device_id={"layer": other}, device_id_type=MESH)
     for load in small:
         load.wait()
     energy[...] = local_energy(spins[...], offdiag[...])
@@ -112,49 +121,52 @@
             device_id_type=MESH,
         )
 
-    def row_copy(m, peer):
+    def row_copy(m, h, peer):
         return pltpu.make_async_remote_copy(
-            src_ref=outgoing.at[m, peer],
-            dst_ref=rows_ref.at[m, :, me],
-            send_sem=row_send.at[m],
-            recv_sem=row_recv.at[m],
+            src_ref=outgoing.at[m, h, peer],
+            dst_ref=rows_ref.at[m, h, me],
+            send_sem=row_send.at[m, h],
+            recv_sem=row_recv.at[m, h],
             device_id={"samp": peer},
             device_id_type=MESH,
         )
 
-    for m in range(mats):
+    def keep(m, h):
+        return pltpu.make_async_copy(outgoing.at[m, h, me], rows_ref.at[m, h, me], own_sem.at[m, h])
+
+    for m, h in parts_of_rows:
         for s in range(samples):
-            for load in loads(m, s):
-                load.wait()
+            if h == 0:
+                for load in loads(m, s):
+                    load.wait()
             jac = lax.dot_general(
-                act[s, m], cot[s, m], (((0,), (0,)), ((), ())), preferred_element_type=f32
+                act[s, m], cot[s, m, :, h * 128 : (h + 1) * 128], (((0,), (0,)), ((), ())),
+                preferred_element_type=f32,
             )
-            for h in range(width // 128):
-                wide[pl.ds(h * width * samples + s, width, stride=samples), :] = jac[:, h * 128 : (h + 1) * 128]
-        for h in range(width // 128):
-            for k in range(peers):
-                start = h * width * samples + k * share * samples
-                block = wide[start : start + share * samples, :]
-                outgoing[m, k, :, :, h * 128 : (h + 1) * 128] = block.reshape(share, samples, 128).astype(jnp.bfloat16)
-        if m == 0:
+            wide[pl.ds(h * width * samples + s, width, stride=samples), :] = jac
+        for k in range(peers):
+            start = h * width * samples + k * share * samples
+            block = wide[start : start + share * samples, :]
+            outgoing[m, h, k] = block.reshape(share, samples, 128).astype(jnp.bfloat16)
+        if (m, h) == (0, 0):
             pl.semaphore_wait(barrier, peers + layers - 2)
             for other in others:
                 pl.semaphore_signal(planes, inc=1, device_id={"layer": other}, device_id_type=MESH)
-        for peer in steps:
-            row_copy(m, peer).start()
-        if m == 0:
-            for peer in steps:
-                energy_copy(peer).start()
-            energy_ref[me] = energy[...]
-        pltpu.make_async_copy(outgoing.at[m, me], rows_ref.at[m, :, me], own_sem.at[m]).start()
+        for peer in steps[::-1] if m == 0 else steps:
+            row_copy(m, h, peer).start()
+        keep(m, h).start()
+    for peer in steps:
+        energy_copy(peer).start()
+    energy_ref[me] = energy[...]
 
     for m in range(mats):
-        pltpu.make_async_copy(outgoing.at[m, me], rows_ref.at[m, :, me], own_sem.at[m]).wait()
-        many = rows_ref.at[m, :, 0 : peers - 1]
-        pltpu.make_async_copy(many, many, row_recv.at[m]).wait()
+        for h in range(halves_of_rows):
+            keep(m, h).wait()
+            many = rows_ref.at[m, h, 0 : peers - 1]
+            pltpu.make_async_copy(many, many, row_recv.at[m, h]).wait()
         left, right = None, None
         for r in range(share):
-            rows = rows_ref[m, r].reshape(peers * samples, width)
+            rows = whole_rows(rows_ref, m, r)
             halves = rows[: peers * samples // 2], rows[peers * samples // 2 :]
             first = products(rows, halves[0])
             second = products(halves[1], halves[1])
@@ -164,7 +176,7 @@
     pl.semaphore_wait(planes, layers - 1)
 
     core = me % 2
-    chip = me // 2 * layers + layer
+    device = me * layers + layer
 
     place = me // 2
 
@@ -173,14 +185,17 @@
 
     def moved(y, z):
         return (place // 4 + y) % 4 * 4 + (place % 4 + z) % 4
+
+    def owning_core(there, plane):
+        return (there * OWNING + plane) % 2
 
     def piece_copy(there, plane):
         return pltpu.make_async_remote_copy(
             src_ref=own_gram.at[tile_at(there, plane)],
-            dst_ref=pieces.at[chip],
+            dst_ref=pieces.at[device],
             send_sem=piece_send,
             recv_sem=piece_recv,
-            device_id={"samp": there * 2 + core, "layer": plane},
+            device_id={"samp": there * 2 + owning_core(there, plane), "layer": plane},
             device_id_type=MESH,
         )
 
@@ -193,43 +208,41 @@
         def _(other=other):
             piece_copy(place, other).start()
 
+    mine = core == owning_core(place, layer)
+
+    @pl.when((layer < OWNING) & jnp.logical_not(mine))
+    def _():
+        piece_copy(place, layer).start()
+
     def await_tiles(sem, ref, count):
         many = ref.at[0 : count * 8]
         pltpu.make_async_copy(many, many, sem).wait()
 
-    owns = layer < OWNING
+    owns = (layer < OWNING) & mine
     tiles = (peers // 2) * OWNING
+    rest = peers * layers - 1
 
     @pl.when(owns)
     def _():
-        pieces[chip] = own_gram[tile_at(place, layer)]
-        many = pieces.at[0 : len(CHIP_STEPS)]
+        pieces[device] = own_gram[tile_at(place, layer)]
+        many = pieces.at[0:rest]
         pltpu.make_async_copy(many, many, piece_recv).wait()
-        sums[core] = jnp.sum(pieces[...], axis=0)
-        sibling = pltpu.make_async_remote_copy(
-            src_ref=sums.at[core],
-            dst_ref=sums.at[core],
-            send_sem=sum_send,
-            recv_sem=sum_recv,
-            device_id={"samp": me + 1 - 2 * core},
-            device_id_type=MESH,
-        )
-        sibling.start()
-        sibling.wait()
-        spread[...] = sums[0] + sums[1]
-        for y, z, x in CHIP_STEPS:
+        spread[...] = jnp.sum(pieces[...], axis=0)
+        targets = [
+            (moved(y, z) * 2 + c, (layer + x) % layers) for y, z, x in CHIP_STEPS for c in range(2)
+        ]
+        for samp, plane in targets + [(me + 1 - 2 * core, layer)]:
             pltpu.make_async_remote_copy(
                 src_ref=spread,
                 dst_ref=gram_ref.at[tile_at(place, layer)],
                 send_sem=spread_send,
                 recv_sem=spread_recv,
-                device_id={"samp": moved(y, z) * 2 + core, "layer": (layer + x) % layers},
+                device_id={"samp": samp, "layer": plane},
                 device_id_type=MESH,
             ).start()
         gram_ref[tile_at(place, layer)] = spread[...]
         await_tiles(piece_send, own_gram, tiles - 1)
         await_tiles(spread_recv, gram_ref, tiles - 1)
-        many = pieces.at[0 : len(CHIP_STEPS)]
         pltpu.make_async_copy(many, many, spread_send).wait()
 
     @pl.when(jnp.logical_not(owns))
@@ -237,9 +250,9 @@
         await_tiles(piece_send, own_gram, tiles)
         await_tiles(spread_recv, gram_ref, tiles)
 
-    for m in range(mats):
-        many = outgoing.at[m, 0 : peers - 1]
-        pltpu.make_async_copy(many, many, row_send.at[m]).wait()
+    for m, h in parts_of_rows:
+        many = outgoing.at[m, h, 0 : peers - 1]
+        pltpu.make_async_copy(many, many, row_send.at[m, h]).wait()
     many = energy_ref.at[0 : peers - 1]
     pltpu.make_async_copy(many, many, energy_send).wait()
     pltpu.make_async_copy(many, many, energy_recv).wait()
@@ -255,7 +268,7 @@
     return pl.pallas_call(
         functools.partial(gram_kernel, peers, layers),
         out_shape=(
-            jax.ShapeDtypeStruct((mats, share, peers, samples, width), bf16),
+            jax.ShapeDtypeStruct((mats, width // 128, peers, share, samples, 128), bf16),
             jax.ShapeDtypeStruct((total // 2 * 3, 128), f32),
             jax.ShapeDtypeStruct((peers, 1, total), f32),
         ),
@@ -267,10 +280,9 @@
             pltpu.VMEM(activations.shape, bf16),
             pltpu.VMEM(cotangents.shape, bf16),
             pltpu.VMEM((width // 128 * width * samples, 128), f32),
-            pltpu.VMEM((mats, peers, share, samples, width), bf16),
+            pltpu.VMEM((mats, width // 128, peers, share, samples, 128), bf16),
             pltpu.VMEM((total // 2 * 3, 128), f32),
-            pltpu.VMEM((peers // 2 * layers, 8, 128), f32),
-            pltpu.VMEM((2, 8, 128), f32),
+            pltpu.VMEM((peers * layers, 8, 128), f32),
             pltpu.VMEM((8, 128), f32),
             pltpu.VMEM((1, total), f32),
             dma((2,)),
@@ -278,11 +290,9 @@
             dma,
             pltpu.SemaphoreType.REGULAR,
             dma((2, mats, samples)),
-            dma((mats,)),
-            dma((mats,)),
-            dma((mats,)),
-            dma,
-            dma,
+            dma((mats, width // 128)),
+            dma((mats, width // 128)),
+            dma((mats, width // 128)),
             dma,
             dma,
             dma,
@@ -429,7 +439,7 @@
 
 
 def solve_kernel(rows_ref, gram_ref, energy_ref, weights_ref, update_ref, work, lower, scaled_lower, shelf):
-    mats, share, peers, samples, width = rows_ref.shape
+    mats, halves, peers, share, samples, lanes = rows_ref.shape
     total = peers * samples
     me = lax.axis_index("samp")
     half = total // 2
@@ -467,13 +477,14 @@
     ).astype(jnp.bfloat16)
     for m in range(mats):
         for r in range(share):
-            rows = rows_ref[m, r].reshape(total, width)
+            rows = whole_rows(rows_ref, m, r)
             parts = jnp.dot(split, rows, preferred_element_type=f32)
             update_ref[m, r : r + 1, :] = jnp.sum(parts, axis=0, keepdims=True)
 
 
 def solve_and_update(rows, gram, energy):
-    mats, share, peers, samples, width = rows.shape
+    mats, halves, peers, share, samples, lanes = rows.shape
+    width = halves * lanes
     total = peers * samples
     vmem = pl.BlockSpec(memory_space=pltpu.VMEM)
     return pl.pallas_call(

time: 58.2 us -> 57.5 us (0.988)
  Pallas kernels: 57.5 us -> 56.8 us
    pallas_call x1, Pallas kernels: 49.7 us -> 49 us  [gram_and_rows(): pl.pallas_call(functools.partial(gram_kernel, peers, layers), out_shape=(...]
where the time goes in v8:
time: 57.5 us; the launch traced here: 57.4 us
  Pallas kernels  56.8 us (99%)
  between operations  0.64 us (1%)
    pallas_call x1, Pallas kernels, gram_and_rows(): pl.pallas_call(functools.partial(gram_kernel, peers, layers), out_shape=(...  49 us
    pallas_call x1, Pallas kernels, solve_and_update(): pl.pallas_call(solve_kernel, out_shape=(jax.ShapeDtypeStruct((1, samples)...  7.73 us

profile of v8, /device:TPU:1, one launch (start us, length us, event | category | flops | bytes accessed | tf_op | source)
XLA Modules:
  0.0 57.4 jit_solution(14918951534309586235)
XLA Ops:
  0.6 49.0 %shard_map.59 = (bf16[2,2,32,8,8,128]{5,4,3,2,1,0:T(8,128)(2,1)S(1)}, f32[384,128]{1,0:T(8,128)S(1)}, f32[32,1,256]{2,1,0:T(1,128)S(1)}) custom-call(s32[8,256]{1,0:T(8,128)} %spins_hbm.1, f32[1,8]{1,0:T(1,128)} %bitcast.2, bf16[8,2,256,256]{3,2,1,0:T(8,128)(2,1)} %act_hbm.1, bf16[8,2,256,256]{3,2,1,0:T(8,128)(2,1)} %cot_hbm.1), custom_call_target="tpu_custom_call" | custom-call | tf_op jit(solution)/shard_map/pallas_call | solution.py:268
  49.7 7.7 %shard_map.60 = (f32[1,8]{1,0:T(1,128)}, f32[2,8,256]{2,1,0:T(8,128)}) custom-call(bf16[2,2,32,8,8,128]{5,4,3,2,1,0:T(8,128)(2,1)S(1)} %get-tuple-element.7.rows_ref, f32[384,128]{1,0:T(8,128)S(1)} %get-tuple-element.8.gram_ref, f32[32,1,256]{2,1,0:T(1,128)S(1)} %get-tuple-element.9.energy_ref), custom_call_target="tpu_custom_call" | custom-call | tf_op jit(solution)/shard_map/pallas_call | solution.py:490

commit v9 on v8

--- a/solution.py
+++ b/solution.py
@@ -227,7 +227,8 @@
         pieces[device] = own_gram[tile_at(place, layer)]
         many = pieces.at[0:rest]
         pltpu.make_async_copy(many, many, piece_recv).wait()
-        spread[...] = jnp.sum(pieces[...], axis=0)
+        groups = pieces[...].reshape(16, (rest + 1) // 16, 8, 128)
+        spread[...] = jnp.sum(jnp.sum(groups, axis=1), axis=0)
         targets = [
             (moved(y, z) * 2 + c, (layer + x) % layers) for y, z, x in CHIP_STEPS for c in range(2)
         ]

time: 57.5 us -> 57.4 us (level)
  no operation moved by 1% of the time
where the time goes in v9:
time: 57.4 us; the launch traced here: 57.3 us
  Pallas kernels  56.7 us (99%)
  between operations  0.64 us (1%)
    pallas_call x1, Pallas kernels, gram_and_rows(): pl.pallas_call(functools.partial(gram_kernel, peers, layers), out_shape=(...  48.9 us
    pallas_call x1, Pallas kernels, solve_and_update(): pl.pallas_call(solve_kernel, out_shape=(jax.ShapeDtypeStruct((1, samples)...  7.73 us

profile of v9, /device:TPU:1, one launch (start us, length us, event | category | flops | bytes accessed | tf_op | source)
XLA Modules:
  0.0 57.3 jit_solution(54398424958126936)
XLA Ops:
  0.6 48.9 %shard_map.59 = (bf16[2,2,32,8,8,128]{5,4,3,2,1,0:T(8,128)(2,1)S(1)}, f32[384,128]{1,0:T(8,128)S(1)}, f32[32,1,256]{2,1,0:T(1,128)S(1)}) custom-call(s32[8,256]{1,0:T(8,128)} %spins_hbm.1, f32[1,8]{1,0:T(1,128)} %bitcast.2, bf16[8,2,256,256]{3,2,1,0:T(8,128)(2,1)} %act_hbm.1, bf16[8,2,256,256]{3,2,1,0:T(8,128)(2,1)} %cot_hbm.1), custom_call_target="tpu_custom_call" | custom-call | tf_op jit(solution)/shard_map/pallas_call | solution.py:269
  49.6 7.7 %shard_map.60 = (f32[1,8]{1,0:T(1,128)}, f32[2,8,256]{2,1,0:T(8,128)}) custom-call(bf16[2,2,32,8,8,128]{5,4,3,2,1,0:T(8,128)(2,1)S(1)} %get-tuple-element.7.rows_ref, f32[384,128]{1,0:T(8,128)S(1)} %get-tuple-element.8.gram_ref, f32[32,1,256]{2,1,0:T(1,128)S(1)} %get-tuple-element.9.energy_ref), custom_call_target="tpu_custom_call" | custom-call | tf_op jit(solution)/shard_map/pallas_call | solution.py:491
